TPU v7x, 256 devices: a whole 4x4x8 slice. The times are simulated.
256 devices in a mesh: grow: 16 (over x, z_lo, core), cy: 4 (over y), cz: 4 (over z_hi).
Axes of the slice: x: 4, y: 4, z: 8 (z_hi: 4, z_lo: 2; z = z_hi * 2 + z_lo), core: 2. Of those that a mesh axis runs over, the one named last changes fastest.
Arguments:
- labels: int32 [64, 512, 512], P('grow', 'cy', 'cz'), may hold values 0 or 1
- roughness: float32 [64, 512, 512], P('grow', 'cy', 'cz'), may hold values from 0 to 1
- potential: float32 [64, 512, 512], P('grow', 'cy', 'cz'), may hold values from 0 to 1
- displacement: float32 [3, 64, 512, 512], P(None, 'grow', 'cy', 'cz'), may hold values from -1.8 to 1.8
Outputs:
- phase_out: float32 [64, 512, 512], P('grow', 'cy', 'cz')
- potential_out: float32 [64, 512, 512], P('grow', 'cy', 'cz')
- displacement_out: float32 [3, 64, 512, 512], P(None, 'grow', 'cy', 'cz')
All inputs are finite; a program needn't handle non-finite values. No bound on the sum of `labels` on one device may be relied on, other than what follows from the above.
Results may differ from a plain program's by a relative error of at most 0.00002.
Values sent between devices are 32-bit elements; how exact they have to be, the bound alone decides.
A program may use at most 64 MiB of HBM per device.

v0:
```python
import jax
import jax.numpy as jnp
from jax import lax
from jax.sharding import PartitionSpec as P

STEPS = 2
SWEEPS = 3


TAU_P = 0.15
TAU_U = 0.08
SHEAR = 1.0
LAME_FIRST = 1.5
STIFF = 6.5
EIGEN = 0.1
COND_EL = 0.1
COND_LI = 0.9
V_HIGH = 1.0
TIME_STEP = 0.05
REST = 0.5
OMEGA_THIRD = 0.1
RATE = 0.5


def extended(cells, sides, width, closed):
    for axis, dim in sides:
        count = lax.axis_size(axis)
        ends = count if closed else count - 1
        head = lax.slice_in_dim(cells, 0, width, axis=dim)
        tail = lax.slice_in_dim(cells, cells.shape[dim] - width, cells.shape[dim], axis=dim)
        cells = jnp.concatenate(
            [
                lax.ppermute(tail, axis, [(i, (i + 1) % count) for i in range(ends)]),
                cells,
                lax.ppermute(head, axis, [((i + 1) % count, i) for i in range(ends)]),
            ],
            axis=dim,
        )
    return cells


def from_behind(block, axis, distance):
    devices = range(lax.axis_size(axis))
    route = [(i - distance, i) for i in devices if i - distance in devices]
    return lax.ppermute(block, axis, route)


def unit(direction, sign):
    offsets = [0, 0, 0]
    offsets[direction] = sign
    return offsets


def offset(field, offsets):
    lead_dims = field.ndim - 3
    slices = [slice(None)] * lead_dims
    for direction in range(3):
        extent = field.shape[lead_dims + direction]
        slices.append(slice(1 + offsets[direction], extent - 1 + offsets[direction]))
    return field[tuple(slices)]


def centre(field):
    return offset(field, (0, 0, 0))


def laplace(field):
    total = -6.0 * centre(field)
    for direction in range(3):
        total = total + offset(field, unit(direction, 1)) + offset(field, unit(direction, -1))
    return total


def interp(phase):
    return phase * phase * (3.0 - 2.0 * phase)


def interp_slope(phase):
    return 6.0 * phase * (1.0 - phase)


def potential_sweep(potential_pad, conduct_pad):
    here = centre(potential_pad)
    conduct_here = centre(conduct_pad)
    flux = jnp.zeros_like(here)
    for direction in range(3):
        for sign in (1, -1):
            moved = unit(direction, sign)
            flux = flux + 0.5 * (offset(conduct_pad, moved) + conduct_here) * (
                offset(potential_pad, moved) - here
            )
    return here + TAU_P * flux


def cross_term(field, first, second):
    total = jnp.zeros_like(centre(field))
    for sign_first in (1, -1):
        for sign_second in (1, -1):
            offsets = [0, 0, 0]
            offsets[first] = sign_first
            offsets[second] = sign_second
            total = total + sign_first * sign_second * offset(field, offsets)
    return 0.25 * total


def elastic_sweep(disp_pad, interp_pad):
    updated = []
    for component in range(3):
        own = disp_pad[component]
        grad_div = (
            offset(own, unit(component, 1)) - 2.0 * centre(own) + offset(own, unit(component, -1))
        )
        for other in range(3):
            if other != component:
                grad_div = grad_div + cross_term(disp_pad[other], component, other)
        slope = 0.5 * (
            offset(interp_pad, unit(component, 1)) - offset(interp_pad, unit(component, -1))
        )
        force = SHEAR * laplace(own) + (LAME_FIRST + SHEAR) * grad_div - STIFF * EIGEN * slope
        updated.append(centre(own) + TAU_U * force)
    return jnp.stack(updated)


def divergence(disp_pad):
    total = jnp.zeros_like(centre(disp_pad[0]))
    for component in range(3):
        total = total + 0.5 * (
            offset(disp_pad[component], unit(component, 1))
            - offset(disp_pad[component], unit(component, -1))
        )
    return total


def phase_update(phase_pad, potential, div_disp):
    phase = centre(phase_pad)
    trace = STIFF * (div_disp - 3.0 * EIGEN * interp(phase))
    over = potential - REST + OMEGA_THIRD * trace
    drive = jnp.exp(over) - jnp.exp(-over)
    change = (
        laplace(phase_pad)
        - 2.0 * phase * (1.0 - phase) * (1.0 - 2.0 * phase)
        - RATE * interp_slope(phase) * drive
    )
    return phase + TIME_STEP * change


def pin_ends(field, width, slab, low, high):
    if width == 0:
        return field
    lead_dims = field.ndim - 3
    planes = field.shape[lead_dims]
    first = lax.axis_index("grow") * slab - width
    position = first + lax.broadcasted_iota(jnp.int32, (planes, 1, 1), 0)
    limit = slab * lax.axis_size("grow")
    result = jnp.where(position < 0, low, field)
    return jnp.where(position >= limit, high, result)


def column_values(values):
    return jnp.array(values, jnp.float32).reshape(len(values), 1, 1, 1)


def strip(field, count):
    for repeat in range(count):
        field = centre(field)
    return field


def shards(labels, roughness, potential, displacement):
    slab = labels.shape[0]
    rim = SWEEPS + 1
    mark = labels.astype(jnp.float32)
    phase = mark * (1.0 - 0.3 * roughness) + (1.0 - mark) * (0.3 * roughness)
    low_five = column_values([1.0, 0.0, 0.0, 0.0, 0.0])
    high_five = column_values([0.0, V_HIGH, 0.0, 0.0, 0.0])
    for step_index in range(STEPS):
        packed = jnp.concatenate([phase[None], potential[None], displacement], axis=0)
        packed = extended(packed, (("grow", 1),), SWEEPS + 1, False)
        packed = pin_ends(packed, SWEEPS + 1, slab, low_five, high_five)
        packed = extended(packed, (("cy", 2), ("cz", 3)), SWEEPS + 1, True)
        phase_pad = packed[0]
        interp_pad = interp(phase_pad)
        conduct_pad = COND_EL + COND_LI * interp_pad
        pot_pad = strip(packed[1], 1)
        conduct_now = centre(conduct_pad)
        for repeat in range(SWEEPS):
            pot_pad = pin_ends(
                potential_sweep(pot_pad, conduct_now), SWEEPS - 1 - repeat, slab, 0.0, V_HIGH
            )
            if repeat + 1 < SWEEPS:
                conduct_now = centre(conduct_now)
        potential = pot_pad
        disp_pad = packed[2:]
        interp_now = interp_pad
        for repeat in range(SWEEPS):
            disp_pad = pin_ends(
                elastic_sweep(disp_pad, interp_now), SWEEPS - repeat, slab, 0.0, 0.0
            )
            if repeat + 1 < SWEEPS:
                interp_now = centre(interp_now)
        div_disp = divergence(disp_pad)
        displacement = centre(disp_pad)
        phase = phase_update(strip(phase_pad, rim - 1), potential, div_disp)
    stacked = jnp.concatenate([phase[None], potential[None], displacement], axis=0)
    arrived = from_behind(stacked, "grow", -1)
    fresh = jnp.array([0.0, V_HIGH, 0.0, 0.0, 0.0], jnp.float32).reshape(5, 1, 1, 1)
    is_last = lax.axis_index("grow") == lax.axis_size("grow") - 1
    arrived = jnp.where(is_last, fresh, arrived)
    return (arrived[0], arrived[1], arrived[2:])


def solution(mesh):
    placed = (
        P("grow", "cy", "cz"),
        P("grow", "cy", "cz"),
        P("grow", "cy", "cz"),
        P(None, "grow", "cy", "cz"),
    )
    return jax.shard_map(
        shards,
        mesh=mesh,
        in_specs=placed,
        out_specs=(P("grow", "cy", "cz"), P("grow", "cy", "cz"), P(None, "grow", "cy", "cz")),
        check_vma=False,
    )
```

profile of v0, /device:TPU:3, one launch (start us, length us, event | category | flops | bytes accessed | tf_op | source)
XLA Modules:
  0.0 295.4 jit_solution(9919258022537184967)
XLA Ops:
  0.6 1.1 add_bitcast_fusion
  1.8 1.4 pad_maximum_fusion.4
  3.1 4.1 %collective-permute-start = (f32[5,4,128,128]{3,2,1,0:T(8,128)S(1)}, f32[5,4,128,128]{3,2,1,0:T(8,128)}, u32[]{:S(2)}, u32[]{:S(2)}) collective-permute-start(f32[5,4,128,128]{3,2,1,0:T(8,128)S(1)} %pad_maximum_fusion.4), channel_id=1, source_target_pairs={{0,16},{16,32},{32,48},{48,64},{64,80},{80,96},{96,112},{112,128},... | collective-permute-start | bytes 3932168 | tf_op jit(solution)/shard_map/ppermute | solution.py:33
  7.3 1.9 collective-permute-start.1
  9.2 23.4 %collective-permute-done = f32[5,4,128,128]{3,2,1,0:T(8,128)} collective-permute-done((f32[5,4,128,128]{3,2,1,0:T(8,128)S(1)}, f32[5,4,128,128]{3,2,1,0:T(8,128)}, u32[]{:S(2)}, u32[]{:S(2)}) %collective-permute-start) | collective-permute-done | bytes 1310752 | tf_op jit(solution)/shard_map/ppermute | solution.py:33
  32.6 4.5 %collective-permute-done.1 = f32[5,4,128,128]{3,2,1,0:T(8,128)} collective-permute-done((f32[5,4,128,128]{3,2,1,0:T(8,128)S(1)}, f32[5,4,128,128]{3,2,1,0:T(8,128)}, u32[]{:S(2)}, u32[]{:S(2)}) %collective-permute-start.1) | collective-permute-done | bytes 1310752 | tf_op jit(solution)/shard_map/ppermute | solution.py:35
  37.1 2.1 fusion.2
  39.2 1.9 copy-done
  41.2 1.4 collective-permute-start.2
  42.5 1.5 collective-permute-start.3
  44.1 3.0 %collective-permute-done.2 = f32[5,12,4,128]{3,2,1,0:T(4,128)S(1)} collective-permute-done((f32[5,12,4,128]{3,2,1,0:T(4,128)S(1)}, f32[5,12,4,128]{3,2,1,0:T(4,128)S(1)}, u32[]{:S(2)}, u32[]{:S(2)}) %collective-permute-start.2) | collective-permute-done | bytes 122912 | tf_op jit(solution)/shard_map/ppermute | solution.py:33
  47.5 2.5 pad_maximum_fusion.2
  50.0 4.6 %fusion.457 = (f32[5,12,136,4]{3,2,1,0:T(8,128)}, f32[5,12,136,4]{3,2,1,0:T(8,128)}) fusion(f32[5,12,136,128]{3,2,1,0:T(8,128)S(1)} %pad_maximum_fusion.2), kind=kLoop, calls=%fused_computation.800 | loop fusion | bytes 522240 | tf_op jit(solution)/shard_map/slice | solution.py:30
  54.6 3.9 %copy.17 = f32[5,12,136,4]{2,3,1,0:T(4,128)S(1)} copy(f32[5,12,136,4]{3,2,1,0:T(8,128)} %get-tuple-element.32) | data formatting | bytes 261120 | tf_op jit(solution)/shard_map/slice | solution.py:30
  58.5 3.1 %collective-permute-start.4 = (f32[5,12,136,4]{2,3,1,0:T(4,128)S(1)}, f32[5,12,136,4]{2,3,1,0:T(4,128)S(1)}, u32[]{:S(2)}, u32[]{:S(2)}) collective-permute-start(f32[5,12,136,4]{2,3,1,0:T(4,128)S(1)} %copy.17), channel_id=1, source_target_pairs={{0,1},{1,2},{2,3},{3,0},{4,5},{5,6},{6,7},{7,4},{8,9},{9,10},{10,1... | collective-permute-start | bytes 391688 | tf_op jit(solution)/shard_map/ppermute | solution.py:33
  61.6 3.9 %copy.18 = f32[5,12,136,4]{2,3,1,0:T(4,128)S(1)} copy(f32[5,12,136,4]{3,2,1,0:T(8,128)} %get-tuple-element.33) | data formatting | bytes 261120 | tf_op jit(solution)/shard_map/slice | solution.py:29
  65.4 2.8 collective-permute-start.5
  68.2 2.1 collective-permute-done.4
  70.4 2.8 copy.19
  73.1 6.7 %collective-permute-done.5 = f32[5,12,136,4]{2,3,1,0:T(4,128)S(1)} collective-permute-done((f32[5,12,136,4]{2,3,1,0:T(4,128)S(1)}, f32[5,12,136,4]{2,3,1,0:T(4,128)S(1)}, u32[]{:S(2)}, u32[]{:S(2)}) %collective-permute-start.5) | collective-permute-done | bytes 130592 | tf_op jit(solution)/shard_map/ppermute | solution.py:35
  79.8 2.8 copy.20
  82.6 8.0 %pad_maximum_fusion = f32[5,12,136,136]{3,2,1,0:T(8,128)S(1)} fusion(f32[5,12,136,4]{3,2,1,0:T(8,128)} %copy.20, f32[5,12,4,128]{3,2,1,0:T(4,128)S(1)} %collective-permute-done.3, f32[5,12,128,128]{3,2,1,0:T(8,128)} %copy-done, f32[5,12,4,128]{3,2,1,0:T(4,128)S(1)} %collective-permute-done.2, f32[5,12,136,4]{3,2,1,0:T(8,128)} %copy.19), kind=kLoop, calls=%fused_computation | loop fusion | flops 4439040 | bytes 8878080 | tf_op jit(solution)/shard_map/concatenate | solution.py:31
  91.8 5.7 %fusion.95 = f32[1,10,134,134]{3,2,1,0:T(8,128)S(1)} fusion(f32[12,136,136]{2,1,0:T(8,128)S(1)} %get-tuple-element.18, f32[12,136,136]{2,1,0:T(8,128)S(1)} %get-tuple-element.20, f32[12,136,136]{2,1,0:T(8,128)S(1)} %get-tuple-element.21, f32[12,136,136]{2,1,0:T(8,128)S(1)} %get-tuple-element.22), kind=kLoop, calls=%fused_computation.183 | loop fusion | flops 5566360 | bytes 12928320 | tf_op jit(solution)/shard_map/stack | solution.py:121
  97.6 5.5 %fusion.78 = f32[1,10,134,134]{3,2,1,0:T(8,128)S(1)} fusion(f32[12,136,136]{2,1,0:T(8,128)S(1)} %get-tuple-element.18, f32[12,136,136]{2,1,0:T(8,128)S(1)} %get-tuple-element.20, f32[12,136,136]{2,1,0:T(8,128)S(1)} %get-tuple-element.22, f32[12,136,136]{2,1,0:T(8,128)S(1)} %get-tuple-element.21), kind=kLoop, calls=%fused_computation.155 | loop fusion | flops 5566360 | bytes 12928320 | tf_op jit(solution)/shard_map/stack | solution.py:121
  103.1 4.8 %fusion.61 = f32[1,10,134,134]{3,2,1,0:T(8,128)S(1)} fusion(f32[12,136,136]{2,1,0:T(8,128)S(1)} %get-tuple-element.18, f32[12,136,136]{2,1,0:T(8,128)S(1)} %get-tuple-element.21, f32[12,136,136]{2,1,0:T(8,128)S(1)} %get-tuple-element.22, f32[12,136,136]{2,1,0:T(8,128)S(1)} %get-tuple-element.20), kind=kLoop, calls=%fused_computation.127 | loop fusion | flops 5566360 | bytes 12928320 | tf_op jit(solution)/shard_map/stack | solution.py:121
  108.8 4.6 %fusion.214 = f32[1,8,132,132]{3,2,1,0:T(8,128)S(1)} fusion(f32[12,136,136]{2,1,0:T(8,128)S(1)} %get-tuple-element.18, f32[10,134,134]{2,1,0:T(8,128)S(1)} %get-tuple-element.29, f32[10,134,134]{2,1,0:T(8,128)S(1)} %get-tuple-element.30, f32[10,134,134]{2,1,0:T(8,128)S(1)} %get-tuple-element.31), kind=kLoop, calls=%fused_computation.389 | loop fusion | flops 4321152 | bytes 10036224 | tf_op jit(solution)/shard_map/stack | solution.py:121
  113.4 4.4 %fusion.197 = f32[1,8,132,132]{3,2,1,0:T(8,128)S(1)} fusion(f32[12,136,136]{2,1,0:T(8,128)S(1)} %get-tuple-element.18, f32[10,134,134]{2,1,0:T(8,128)S(1)} %get-tuple-element.29, f32[10,134,134]{2,1,0:T(8,128)S(1)} %get-tuple-element.31, f32[10,134,134]{2,1,0:T(8,128)S(1)} %get-tuple-element.30), kind=kLoop, calls=%fused_computation.361 | loop fusion | flops 4321152 | bytes 10036224 | tf_op jit(solution)/shard_map/stack | solution.py:121
  117.8 4.1 %fusion.180 = f32[1,8,132,132]{3,2,1,0:T(8,128)S(1)} fusion(f32[12,136,136]{2,1,0:T(8,128)S(1)} %get-tuple-element.18, f32[10,134,134]{2,1,0:T(8,128)S(1)} %get-tuple-element.30, f32[10,134,134]{2,1,0:T(8,128)S(1)} %get-tuple-element.31, f32[10,134,134]{2,1,0:T(8,128)S(1)} %get-tuple-element.29), kind=kLoop, calls=%fused_computation.333 | loop fusion | flops 4321152 | bytes 10036224 | tf_op jit(solution)/shard_map/stack | solution.py:121
  122.5 3.2 %fusion.354 = f32[1,6,130,130]{3,2,1,0:T(8,128)S(1)} fusion(f32[12,136,136]{2,1,0:T(8,128)S(1)} %get-tuple-element.18, f32[8,132,132]{2,1,0:T(8,128)S(1)} %get-tuple-element.41, f32[8,132,132]{2,1,0:T(8,128)S(1)} %get-tuple-element.42, f32[8,132,132]{2,1,0:T(8,128)S(1)} %get-tuple-element.43), kind=kLoop, calls=%fused_computation.625 | loop fusion | flops 3143400 | bytes 7300800 | tf_op jit(solution)/shard_map/stack | solution.py:121
  125.7 3.1 %fusion.337 = f32[1,6,130,130]{3,2,1,0:T(8,128)S(1)} fusion(f32[12,136,136]{2,1,0:T(8,128)S(1)} %get-tuple-element.18, f32[8,132,132]{2,1,0:T(8,128)S(1)} %get-tuple-element.41, f32[8,132,132]{2,1,0:T(8,128)S(1)} %get-tuple-element.43, f32[8,132,132]{2,1,0:T(8,128)S(1)} %get-tuple-element.42), kind=kLoop, calls=%fused_computation.597 | loop fusion | flops 3143400 | bytes 7300800 | tf_op jit(solution)/shard_map/stack | solution.py:121
  128.9 2.8 fusion.320
  132.5 4.6 %fusion.230 = f32[8,132,132]{2,1,0:T(8,128)S(1)} fusion(f32[12,136,136]{2,1,0:T(8,128)S(1)} %get-tuple-element.19, f32[12,136,136]{2,1,0:T(8,128)S(1)} %get-tuple-element.17, pred[8]{0:T(512)(128)(4,1)S(1)} %get-tuple-element.56, pred[8]{0:T(512)(128)(4,1)S(1)} %get-tuple-element.57), kind=kLoop, calls=%fused_computation.416 | loop fusion | flops 4599936 | bytes 8363536 | tf_op jit(solution)/shard_map/jit(_where)/select_n | solution.py:156
  137.1 2.9 fusion.370
  140.0 1.8 fusion.445
  141.9 5.1 %collective-permute-start.6 = (f32[5,4,128,128]{3,2,1,0:T(8,128)S(1)}, f32[5,4,128,128]{3,2,1,0:T(8,128)S(1)}, u32[]{:S(2)}, u32[]{:S(2)}) collective-permute-start(f32[5,4,128,128]{3,2,1,0:T(8,128)S(1)} %pad_maximum_fusion.5), channel_id=1, source_target_pairs={{0,16},{16,32},{32,48},{48,64},{64,80},{80,96},{96,112},{112,128},... | collective-permute-start | bytes 3932168 | tf_op jit(solution)/shard_map/ppermute | solution.py:33
  147.0 1.9 collective-permute-start.7
  148.9 24.4 %collective-permute-done.6 = f32[5,4,128,128]{3,2,1,0:T(8,128)S(1)} collective-permute-done((f32[5,4,128,128]{3,2,1,0:T(8,128)S(1)}, f32[5,4,128,128]{3,2,1,0:T(8,128)S(1)}, u32[]{:S(2)}, u32[]{:S(2)}) %collective-permute-start.6) | collective-permute-done | bytes 1310752 | tf_op jit(solution)/shard_map/ppermute | solution.py:33
  173.3 3.6 %collective-permute-done.7 = f32[5,4,128,128]{3,2,1,0:T(8,128)S(1)} collective-permute-done((f32[5,4,128,128]{3,2,1,0:T(8,128)S(1)}, f32[5,4,128,128]{3,2,1,0:T(8,128)S(1)}, u32[]{:S(2)}, u32[]{:S(2)}) %collective-permute-start.7) | collective-permute-done | bytes 1310752 | tf_op jit(solution)/shard_map/ppermute | solution.py:35
  177.7 1.4 collective-permute-start.8
  179.1 1.4 collective-permute-start.9
  180.5 3.1 %collective-permute-done.8 = f32[5,12,4,128]{3,2,1,0:T(4,128)S(1)} collective-permute-done((f32[5,12,4,128]{3,2,1,0:T(4,128)S(1)}, f32[5,12,4,128]{3,2,1,0:T(4,128)S(1)}, u32[]{:S(2)}, u32[]{:S(2)}) %collective-permute-start.8) | collective-permute-done | bytes 122912 | tf_op jit(solution)/shard_map/ppermute | solution.py:33
  184.6 4.6 %fusion.456 = (f32[5,12,136,4]{3,2,1,0:T(8,128)}, f32[5,12,136,4]{3,2,1,0:T(8,128)}) fusion(f32[5,12,136,128]{3,2,1,0:T(8,128)S(1)} %pad_maximum_fusion.3), kind=kLoop, calls=%fused_computation.799 | loop fusion | bytes 522240 | tf_op jit(solution)/shard_map/slice | solution.py:30
  189.2 3.9 %copy.21 = f32[5,12,136,4]{2,3,1,0:T(4,128)S(1)} copy(f32[5,12,136,4]{3,2,1,0:T(8,128)} %get-tuple-element.27) | data formatting | bytes 261120 | tf_op jit(solution)/shard_map/slice | solution.py:30
  193.0 2.9 collective-permute-start.10
  195.9 3.9 %copy.22 = f32[5,12,136,4]{2,3,1,0:T(4,128)S(1)} copy(f32[5,12,136,4]{3,2,1,0:T(8,128)} %get-tuple-element.28) | data formatting | bytes 261120 | tf_op jit(solution)/shard_map/slice | solution.py:29
  200.8 5.1 %collective-permute-done.10 = f32[5,12,136,4]{2,3,1,0:T(4,128)S(1)} collective-permute-done((f32[5,12,136,4]{2,3,1,0:T(4,128)S(1)}, f32[5,12,136,4]{2,3,1,0:T(4,128)S(1)}, u32[]{:S(2)}, u32[]{:S(2)}) %collective-permute-start.10) | collective-permute-done | bytes 130592 | tf_op jit(solution)/shard_map/ppermute | solution.py:33
  205.9 2.8 copy.23
  208.6 3.5 %collective-permute-done.11 = f32[5,12,136,4]{2,3,1,0:T(4,128)S(1)} collective-permute-done((f32[5,12,136,4]{2,3,1,0:T(4,128)S(1)}, f32[5,12,136,4]{2,3,1,0:T(4,128)S(1)}, u32[]{:S(2)}, u32[]{:S(2)}) %collective-permute-start.11) | collective-permute-done | bytes 130592 | tf_op jit(solution)/shard_map/ppermute | solution.py:35
  212.2 2.8 copy.24
  215.0 8.0 %pad_maximum_fusion.1 = f32[5,12,136,136]{3,2,1,0:T(8,128)S(1)} fusion(f32[5,12,136,4]{3,2,1,0:T(8,128)} %copy.24, f32[5,12,4,128]{3,2,1,0:T(4,128)S(1)} %collective-permute-done.9, f32[5,12,128,128]{3,2,1,0:T(8,128)} %copy-done.1, f32[5,12,4,128]{3,2,1,0:T(4,128)S(1)} %collective-permute-done.8, f32[5,12,136,4]{3,2,1,0:T(8,128)} %copy.23), kind=kLoop, calls=%fused_computation.1 | loop fusion | flops 4439040 | bytes 8878080 | tf_op jit(solution)/shard_map/concatenate | solution.py:31
  224.2 5.7 %fusion.46 = f32[1,10,134,134]{3,2,1,0:T(8,128)S(1)} fusion(f32[12,136,136]{2,1,0:T(8,128)S(1)} %get-tuple-element.11, f32[12,136,136]{2,1,0:T(8,128)S(1)} %get-tuple-element.13, f32[12,136,136]{2,1,0:T(8,128)S(1)} %get-tuple-element.14, f32[12,136,136]{2,1,0:T(8,128)S(1)} %get-tuple-element.15), kind=kLoop, calls=%fused_computation.98 | loop fusion | flops 5566360 | bytes 12928320 | tf_op jit(solution)/shard_map/stack | solution.py:121
  230.0 5.5 %fusion.29 = f32[1,10,134,134]{3,2,1,0:T(8,128)S(1)} fusion(f32[12,136,136]{2,1,0:T(8,128)S(1)} %get-tuple-element.11, f32[12,136,136]{2,1,0:T(8,128)S(1)} %get-tuple-element.13, f32[12,136,136]{2,1,0:T(8,128)S(1)} %get-tuple-element.15, f32[12,136,136]{2,1,0:T(8,128)S(1)} %get-tuple-element.14), kind=kLoop, calls=%fused_computation.70 | loop fusion | flops 5566360 | bytes 12928320 | tf_op jit(solution)/shard_map/stack | solution.py:121
  235.5 4.9 %fusion.12 = f32[1,10,134,134]{3,2,1,0:T(8,128)S(1)} fusion(f32[12,136,136]{2,1,0:T(8,128)S(1)} %get-tuple-element.11, f32[12,136,136]{2,1,0:T(8,128)S(1)} %get-tuple-element.14, f32[12,136,136]{2,1,0:T(8,128)S(1)} %get-tuple-element.15, f32[12,136,136]{2,1,0:T(8,128)S(1)} %get-tuple-element.13), kind=kLoop, calls=%fused_computation.42 | loop fusion | flops 5566360 | bytes 12928320 | tf_op jit(solution)/shard_map/stack | solution.py:121
  241.2 4.6 %fusion.144 = f32[1,8,132,132]{3,2,1,0:T(8,128)S(1)} fusion(f32[12,136,136]{2,1,0:T(8,128)S(1)} %get-tuple-element.11, f32[10,134,134]{2,1,0:T(8,128)S(1)} %get-tuple-element.24, f32[10,134,134]{2,1,0:T(8,128)S(1)} %get-tuple-element.25, f32[10,134,134]{2,1,0:T(8,128)S(1)} %get-tuple-element.26), kind=kLoop, calls=%fused_computation.271 | loop fusion | flops 4321152 | bytes 10036224 | tf_op jit(solution)/shard_map/stack | solution.py:121
  245.8 4.4 %fusion.127 = f32[1,8,132,132]{3,2,1,0:T(8,128)S(1)} fusion(f32[12,136,136]{2,1,0:T(8,128)S(1)} %get-tuple-element.11, f32[10,134,134]{2,1,0:T(8,128)S(1)} %get-tuple-element.24, f32[10,134,134]{2,1,0:T(8,128)S(1)} %get-tuple-element.26, f32[10,134,134]{2,1,0:T(8,128)S(1)} %get-tuple-element.25), kind=kLoop, calls=%fused_computation.243 | loop fusion | flops 4321152 | bytes 10036224 | tf_op jit(solution)/shard_map/stack | solution.py:121
  250.2 4.2 %fusion.110 = f32[1,8,132,132]{3,2,1,0:T(8,128)S(1)} fusion(f32[12,136,136]{2,1,0:T(8,128)S(1)} %get-tuple-element.11, f32[10,134,134]{2,1,0:T(8,128)S(1)} %get-tuple-element.25, f32[10,134,134]{2,1,0:T(8,128)S(1)} %get-tuple-element.26, f32[10,134,134]{2,1,0:T(8,128)S(1)} %get-tuple-element.24), kind=kLoop, calls=%fused_computation.215 | loop fusion | flops 4321152 | bytes 10036224 | tf_op jit(solution)/shard_map/stack | solution.py:121
  255.1 3.2 %fusion.284 = f32[1,6,130,130]{3,2,1,0:T(8,128)S(1)} fusion(f32[12,136,136]{2,1,0:T(8,128)S(1)} %get-tuple-element.11, f32[8,132,132]{2,1,0:T(8,128)S(1)} %get-tuple-element.38, f32[8,132,132]{2,1,0:T(8,128)S(1)} %get-tuple-element.39, f32[8,132,132]{2,1,0:T(8,128)S(1)} %get-tuple-element.40), kind=kLoop, calls=%fused_computation.507 | loop fusion | flops 3143400 | bytes 7300800 | tf_op jit(solution)/shard_map/stack | solution.py:121
  258.3 3.1 %fusion.267 = f32[1,6,130,130]{3,2,1,0:T(8,128)S(1)} fusion(f32[12,136,136]{2,1,0:T(8,128)S(1)} %get-tuple-element.11, f32[8,132,132]{2,1,0:T(8,128)S(1)} %get-tuple-element.38, f32[8,132,132]{2,1,0:T(8,128)S(1)} %get-tuple-element.40, f32[8,132,132]{2,1,0:T(8,128)S(1)} %get-tuple-element.39), kind=kLoop, calls=%fused_computation.479 | loop fusion | flops 3143400 | bytes 7300800 | tf_op jit(solution)/shard_map/stack | solution.py:121
  261.5 2.8 fusion.250
  265.1 4.4 %fusion.160 = f32[8,132,132]{2,1,0:T(8,128)S(1)} fusion(f32[12,136,136]{2,1,0:T(8,128)S(1)} %get-tuple-element.12, f32[12,136,136]{2,1,0:T(8,128)S(1)} %get-tuple-element.10, pred[8]{0:T(512)(128)(4,1)S(1)} %get-tuple-element.56, pred[8]{0:T(512)(128)(4,1)S(1)} %get-tuple-element.57), kind=kLoop, calls=%fused_computation.298 | loop fusion | flops 4599936 | bytes 8363536 | tf_op jit(solution)/shard_map/jit(_where)/select_n | solution.py:156
  269.5 2.9 fusion.300
  272.4 1.8 fusion.415
  274.3 3.2 %collective-permute-start.12 = (f32[5,4,128,128]{3,2,1,0:T(8,128)S(1)}, f32[5,4,128,128]{3,2,1,0:T(8,128)S(1)}, u32[]{:S(2)}, u32[]{:S(2)}) collective-permute-start(f32[5,4,128,128]{3,2,1,0:T(8,128)S(1)} %pad_maximum_fusion.6), channel_id=1, source_target_pairs={{16,0},{32,16},{48,32},{64,48},{80,64},{96,80},{112,96},{128,112},... | collective-permute-start | bytes 3932168 | tf_op jit(solution)/shard_map/ppermute | solution.py:45
  277.6 15.7 %collective-permute-done.12 = f32[5,4,128,128]{3,2,1,0:T(8,128)S(1)} collective-permute-done((f32[5,4,128,128]{3,2,1,0:T(8,128)S(1)}, f32[5,4,128,128]{3,2,1,0:T(8,128)S(1)}, u32[]{:S(2)}, u32[]{:S(2)}) %collective-permute-start.12) | collective-permute-done | bytes 1310752 | tf_op jit(solution)/shard_map/ppermute | solution.py:45
  (45 shorter events, 12.4 us)
Async XLA Ops:
  1.7 35.4 %copy-start.2 = (f32[3,4,128,128]{3,2,1,0:T(8,128)S(1)}, f32[3,4,128,128]{3,2,1,0:T(8,128)}, u32[]{:S(2)}) copy-start(f32[3,4,128,128]{3,2,1,0:T(8,128)} %param.10) | copy-start | bytes 2359300
  1.7 35.4 %copy-start.3 = (f32[4,128,128]{2,1,0:T(8,128)S(1)}, f32[4,128,128]{2,1,0:T(8,128)}, u32[]{:S(2)}) copy-start(f32[4,128,128]{2,1,0:T(8,128)} %param.9) | copy-start | bytes 786436
  1.8 35.4 %copy-start.4 = (f32[5]{0:T(128)S(1)}, f32[5]{0:T(128)}, u32[]{:S(2)}) copy-start(f32[5]{0:T(128)} %constant.119.clone) | copy-start | bytes 64
  1.8 35.4 %copy-start.5 = (f32[5]{0:T(128)S(1)}, f32[5]{0:T(128)}, u32[]{:S(2)}) copy-start(f32[5]{0:T(128)} %constant.118.clone) | copy-start | bytes 64
  3.1 29.5 %collective-permute-start = (f32[5,4,128,128]{3,2,1,0:T(8,128)S(1)}, f32[5,4,128,128]{3,2,1,0:T(8,128)}, u32[]{:S(2)}, u32[]{:S(2)}) collective-permute-start(f32[5,4,128,128]{3,2,1,0:T(8,128)S(1)} %pad_maximum_fusion.4), channel_id=1, source_target_pairs={{0,16},{16,32},{32,48},{48,64},{64,80},{80,96},{96,112},{112,128},... | collective-permute-start | bytes 3932168 | tf_op jit(solution)/shard_map/ppermute | solution.py:33
  7.3 29.9 %collective-permute-start.1 = (f32[5,4,128,128]{3,2,1,0:T(8,128)S(1)}, f32[5,4,128,128]{3,2,1,0:T(8,128)}, u32[]{:S(2)}, u32[]{:S(2)}) collective-permute-start(f32[5,4,128,128]{3,2,1,0:T(8,128)S(1)} %pad_maximum_fusion.4), channel_id=1, source_target_pairs={{16,0},{32,16},{48,32},{64,48},{80,64},{96,80},{112,96},{128,112},... | collective-permute-start | bytes 3932168 | tf_op jit(solution)/shard_map/ppermute | solution.py:35
  39.2 1.9 copy-start
  41.2 5.9 %collective-permute-start.2 = (f32[5,12,4,128]{3,2,1,0:T(4,128)S(1)}, f32[5,12,4,128]{3,2,1,0:T(4,128)S(1)}, u32[]{:S(2)}, u32[]{:S(2)}) collective-permute-start(f32[5,12,4,128]{3,2,1,0:T(4,128)S(1)} %get-tuple-element.36), channel_id=1, source_target_pairs={{0,4},{4,8},{8,12},{12,0},{1,5},{5,9},{9,13},{13,1},{2,6},{6,10},{... | collective-permute-start | bytes 368648 | tf_op jit(solution)/shard_map/ppermute | solution.py:33
  42.5 5.0 %collective-permute-start.3 = (f32[5,12,4,128]{3,2,1,0:T(4,128)S(1)}, f32[5,12,4,128]{3,2,1,0:T(4,128)S(1)}, u32[]{:S(2)}, u32[]{:S(2)}) collective-permute-start(f32[5,12,4,128]{3,2,1,0:T(4,128)S(1)} %get-tuple-element.37), channel_id=1, source_target_pairs={{4,0},{8,4},{12,8},{0,12},{5,1},{9,5},{13,9},{1,13},{6,2},{10,6},{... | collective-permute-start | bytes 368648 | tf_op jit(solution)/shard_map/ppermute | solution.py:35
  58.5 11.9 %collective-permute-start.4 = (f32[5,12,136,4]{2,3,1,0:T(4,128)S(1)}, f32[5,12,136,4]{2,3,1,0:T(4,128)S(1)}, u32[]{:S(2)}, u32[]{:S(2)}) collective-permute-start(f32[5,12,136,4]{2,3,1,0:T(4,128)S(1)} %copy.17), channel_id=1, source_target_pairs={{0,1},{1,2},{2,3},{3,0},{4,5},{5,6},{6,7},{7,4},{8,9},{9,10},{10,1... | collective-permute-start | bytes 391688 | tf_op jit(solution)/shard_map/ppermute | solution.py:33
  65.4 14.4 %collective-permute-start.5 = (f32[5,12,136,4]{2,3,1,0:T(4,128)S(1)}, f32[5,12,136,4]{2,3,1,0:T(4,128)S(1)}, u32[]{:S(2)}, u32[]{:S(2)}) collective-permute-start(f32[5,12,136,4]{2,3,1,0:T(4,128)S(1)} %copy.18), channel_id=1, source_target_pairs={{1,0},{2,1},{3,2},{0,3},{5,4},{6,5},{7,6},{4,7},{9,8},{10,9},{11,1... | collective-permute-start | bytes 391688 | tf_op jit(solution)/shard_map/ppermute | solution.py:35
  141.9 31.4 %collective-permute-start.6 = (f32[5,4,128,128]{3,2,1,0:T(8,128)S(1)}, f32[5,4,128,128]{3,2,1,0:T(8,128)S(1)}, u32[]{:S(2)}, u32[]{:S(2)}) collective-permute-start(f32[5,4,128,128]{3,2,1,0:T(8,128)S(1)} %pad_maximum_fusion.5), channel_id=1, source_target_pairs={{0,16},{16,32},{32,48},{48,64},{64,80},{80,96},{96,112},{112,128},... | collective-permute-start | bytes 3932168 | tf_op jit(solution)/shard_map/ppermute | solution.py:33
  147.0 29.9 %collective-permute-start.7 = (f32[5,4,128,128]{3,2,1,0:T(8,128)S(1)}, f32[5,4,128,128]{3,2,1,0:T(8,128)S(1)}, u32[]{:S(2)}, u32[]{:S(2)}) collective-permute-start(f32[5,4,128,128]{3,2,1,0:T(8,128)S(1)} %pad_maximum_fusion.5), channel_id=1, source_target_pairs={{16,0},{32,16},{48,32},{64,48},{80,64},{96,80},{112,96},{128,112},... | collective-permute-start | bytes 3932168 | tf_op jit(solution)/shard_map/ppermute | solution.py:35
  177.6 6.3 %copy-start.1 = (f32[5,12,128,128]{3,2,1,0:T(8,128)}, f32[5,12,128,128]{3,2,1,0:T(8,128)S(1)}, u32[]{:S(2)}) copy-start(f32[5,12,128,128]{3,2,1,0:T(8,128)S(1)} %fusion.3) | copy-start | bytes 11796484
  177.7 5.8 %collective-permute-start.8 = (f32[5,12,4,128]{3,2,1,0:T(4,128)S(1)}, f32[5,12,4,128]{3,2,1,0:T(4,128)S(1)}, u32[]{:S(2)}, u32[]{:S(2)}) collective-permute-start(f32[5,12,4,128]{3,2,1,0:T(4,128)S(1)} %get-tuple-element.34), channel_id=1, source_target_pairs={{0,4},{4,8},{8,12},{12,0},{1,5},{5,9},{9,13},{13,1},{2,6},{6,10},{... | collective-permute-start | bytes 368648 | tf_op jit(solution)/shard_map/ppermute | solution.py:33
  179.1 4.9 %collective-permute-start.9 = (f32[5,12,4,128]{3,2,1,0:T(4,128)S(1)}, f32[5,12,4,128]{3,2,1,0:T(4,128)S(1)}, u32[]{:S(2)}, u32[]{:S(2)}) collective-permute-start(f32[5,12,4,128]{3,2,1,0:T(4,128)S(1)} %get-tuple-element.35), channel_id=1, source_target_pairs={{4,0},{8,4},{12,8},{0,12},{5,1},{9,5},{13,9},{1,13},{6,2},{10,6},{... | collective-permute-start | bytes 368648 | tf_op jit(solution)/shard_map/ppermute | solution.py:35
  193.0 12.8 %collective-permute-start.10 = (f32[5,12,136,4]{2,3,1,0:T(4,128)S(1)}, f32[5,12,136,4]{2,3,1,0:T(4,128)S(1)}, u32[]{:S(2)}, u32[]{:S(2)}) collective-permute-start(f32[5,12,136,4]{2,3,1,0:T(4,128)S(1)} %copy.21), channel_id=1, source_target_pairs={{0,1},{1,2},{2,3},{3,0},{4,5},{5,6},{6,7},{7,4},{8,9},{9,10},{10,1... | collective-permute-start | bytes 391688 | tf_op jit(solution)/shard_map/ppermute | solution.py:33
  199.8 12.4 %collective-permute-start.11 = (f32[5,12,136,4]{2,3,1,0:T(4,128)S(1)}, f32[5,12,136,4]{2,3,1,0:T(4,128)S(1)}, u32[]{:S(2)}, u32[]{:S(2)}) collective-permute-start(f32[5,12,136,4]{2,3,1,0:T(4,128)S(1)} %copy.22), channel_id=1, source_target_pairs={{1,0},{2,1},{3,2},{0,3},{5,4},{6,5},{7,6},{4,7},{9,8},{10,9},{11,1... | collective-permute-start | bytes 391688 | tf_op jit(solution)/shard_map/ppermute | solution.py:35
  274.3 18.9 %collective-permute-start.12 = (f32[5,4,128,128]{3,2,1,0:T(8,128)S(1)}, f32[5,4,128,128]{3,2,1,0:T(8,128)S(1)}, u32[]{:S(2)}, u32[]{:S(2)}) collective-permute-start(f32[5,4,128,128]{3,2,1,0:T(8,128)S(1)} %pad_maximum_fusion.6), channel_id=1, source_target_pairs={{16,0},{32,16},{48,32},{64,48},{80,64},{96,80},{112,96},{128,112},... | collective-permute-start | bytes 3932168 | tf_op jit(solution)/shard_map/ppermute | solution.py:45
where the time goes:
time: 301 us; the launch traced here: 295 us
  other arithmetic  123 us (41%)
  waiting for transfers between devices  96 us (32%)
  local copies, waits for them, and re-layouts  43.1 us (14%)
  starting transfers between devices  31.7 us (11%)
    another operation x18, other arithmetic, elastic_sweep(): return jnp.stack(updated)  76.8 us
    ppermute x6, waiting for transfers between devices, extended(): lax.ppermute(tail, axis, [(i, (i + 1) % count) for i in range(ends)])  61.1 us
    select_n x12, other arithmetic, pin_ends(): return jnp.where(position >= limit, high, result)  20.2 us
    ppermute x6, waiting for transfers between devices, extended(): lax.ppermute(head, axis, [((i + 1) % count, i) for i in range(ends)])  19.2 us
    concatenate x4, other arithmetic, extended(): jnp.concatenate([lax.ppermute(tail, axis, [(i, (i + 1) % count) for i in...  19.1 us
    ppermute x6, starting transfers between devices, extended(): lax.ppermute(tail, axis, [(i, (i + 1) % count) for i in range(ends)])  17.9 us
    slice x6, local copies, waits for them, and re-layouts, extended(): lax.slice_in_dim(cells, cells.shape[dim] - width, cells.shape[dim], axis=...  17 us
    ppermute x1, waiting for transfers between devices, from_behind(): return lax.ppermute(block, axis, route)  15.7 us
  transfers between devices with their start and end apart: 13, of which 13 were waited for; matrix products, arithmetic and copies ran while one was open for 5% of the time, Pallas kernels for 0%

commit v1 on v0

v1 whole, which is shorter than its diff:
```python
import functools

import jax
import jax.numpy as jnp
from jax import lax
from jax.experimental import pallas as pl
from jax.experimental.pallas import tpu as pltpu
from jax.sharding import PartitionSpec as P

MESH = pl.DeviceIdType.MESH
LANES = 128
TOP = 8
CHUNK = 32
LEVELS = 7
COPIES = 160


class Wires:
    def __init__(self, send_sem, recv_sem, place):
        self.send_sem, self.recv_sem = send_sem, recv_sem
        self.g, self.y, self.z, self.ng, self.ny, self.nz = place
        self.count = 0
        self.pending = []

    def send(self, src, dst, dg, dy, dz):
        index = self.count
        self.count += 1
        target = (
            self.g + dg,
            lax.rem(self.y + dy + self.ny, self.ny),
            lax.rem(self.z + dz + self.nz, self.nz),
        )
        copy = pltpu.make_async_remote_copy(
            src_ref=src,
            dst_ref=dst,
            send_sem=self.send_sem.at[index],
            recv_sem=self.recv_sem.at[index],
            device_id=target,
            device_id_type=MESH,
        )
        self.when_valid(dg, copy.start)
        self.pending.append((dg, copy))
        return (dg, copy)

    def when_valid(self, dg, action):
        if dg == 0:
            action()
        else:
            ok = self.g + dg >= 0 if dg < 0 else self.g + dg < self.ng
            pl.when(ok)(action)

    def receive(self, messages):
        for dg, copy in messages:
            self.when_valid(-dg, copy.wait_recv)

    def drain(self):
        for dg, copy in self.pending:
            self.when_valid(dg, copy.wait_send)


def kernel(
    ng, ny, nz,
    lab, rough, pot, disp,
    ph_out, pot_out, u_out,
    UE, CE, RCU, SCU, PH, RCP, SCP,
    HH, CC, GZ, CZP, CZM, PZ, ZB, SB, PZP, PZM, TS, TT, HT,
    send_sem, recv_sem,
):
    g, y, z = lax.axis_index("grow"), lax.axis_index("cy"), lax.axis_index("cz")
    wires = Wires(send_sem, recv_sem, (g, y, z, ng, ny, nz))
    slab = lab.shape[0]
    rows = lab.shape[1]
    low, high = TOP - 1, TOP + rows
    own = slice(TOP, TOP + rows)
    pairs = 4 * slab

    barrier = pltpu.get_barrier_semaphore()
    around = [(a, b) for a in (-1, 0, 1) for b in (-1, 0, 1)]
    partners = [(0, a, b) for a, b in around if (a, b) != (0, 0)]
    partners += [(s, a, b) for s in (-1, 1) for a, b in around]
    partners += [(-2, 0, 0), (2, 0, 0)]
    for dg, dy, dz in partners:
        def greet(dg=dg, dy=dy, dz=dz):
            pl.semaphore_signal(
                barrier,
                inc=1,
                device_id=(
                    g + dg,
                    lax.rem(y + dy + ny, ny),
                    lax.rem(z + dz + nz, nz),
                ),
                device_id_type=MESH,
            )
        wires.when_valid(dg, greet)

    for c in range(3):
        for p in range(slab):
            UE[0, c, 1 + p, own, :] = disp[c, p]
    for p in range(slab):
        UE[0, 3, 1 + p, own, :] = pot[p]
        mark = lab[p].astype(jnp.float32)
        part = 0.3 * rough[p]
        PH[0, 1 + p, own, :] = mark * (1.0 - part) + (1.0 - mark) * part

    plane_shape = UE.shape[3:]

    @pl.when(g == 0)
    def _():
        for level in range(4):
            for f in range(4):
                UE[level, f, 0] = jnp.zeros(plane_shape, jnp.float32)
            RCU[level, 2] = jnp.zeros(RCU.shape[2:], jnp.float32)
        PH[0, 0] = jnp.ones(plane_shape, jnp.float32)

    @pl.when(g == ng - 1)
    def _():
        for level in range(LEVELS):
            for f in range(4):
                value = 1.0 if f == 3 else 0.0
                for p in (5, 6):
                    UE[level, f, p] = jnp.full(plane_shape, value, jnp.float32)
            CE[level, :, :, 4] = jnp.zeros((2, 3, 16, LANES), jnp.float32)
            for side in range(2):
                RCU[level, 1, side, 0 : 3 * slab] = jnp.zeros((3 * slab, LANES), jnp.float32)
                RCU[level, 1, side, 3 * slab : pairs] = jnp.ones((slab, LANES), jnp.float32)
        PH[0, 5] = jnp.zeros(plane_shape, jnp.float32)
        for p in range(5, 10):
            PH[1, p] = jnp.zeros(plane_shape, jnp.float32)
        RCP[1, 1] = jnp.zeros(RCP.shape[2:], jnp.float32)

    @pl.when(g == ng - 2)
    def _():
        PH[1, 9] = jnp.zeros(plane_shape, jnp.float32)

    lane = lax.broadcasted_iota(jnp.int32, (CHUNK, LANES), 1)
    lane_row = lax.broadcasted_iota(jnp.int32, (1, LANES), 1)
    chunks = [(TOP + start, start) for start in range(0, rows, CHUNK)]

    def pack(planes):
        for at, start in chunks:
            tile = None
            for k, (ref, index) in enumerate(planes):
                moved = pltpu.roll(ref[index + (pl.ds(at, CHUNK), slice(None))], 2 * k + 1, 1)
                tile = moved if tile is None else jnp.where(lane // 2 == k, moved, tile)
            TS[pl.ds(start, CHUNK), :] = tile
        TT[...] = jnp.transpose(TS[...])

    def send_level(level, slide):
        pack([(UE, (level, f, 1 + p)) for f in range(4) for p in range(slab)])
        SCU[level, 1] = TT[pl.ds(0, pairs, stride=2), :]
        SCU[level, 0] = TT[pl.ds(1, pairs, stride=2), :]
        edge = ((-1, TOP, high), (1, TOP + rows - 1, low))
        flat, far = [], []

        def row(dy, fields, here, there, dg):
            (_, src, dst) = edge[0] if dy < 0 else edge[1]
            return wires.send(
                UE.at[level, fields, here, pl.ds(src, 1)],
                UE.at[level, fields, there, pl.ds(dst, 1)],
                dg, dy, 0,
            )

        def corner(dy, dz, here, there, dg):
            src, dst = (TOP, TOP) if dy < 0 else (TOP + rows - 1, TOP - 1)
            return wires.send(
                UE.at[level, pl.ds(0, 3), here, pl.ds(src, 1)],
                CE.at[level, 0 if dz > 0 else 1, :, there, pl.ds(dst, 1)],
                dg, dy, dz,
            )

        def column(dz, slot, dg):
            return wires.send(
                SCU.at[level, 0 if dz < 0 else 1],
                RCU.at[level, slot, 1 if dz < 0 else 0],
                dg, 0, dz,
            )

        every = pl.ds(0, 4)
        mine = pl.ds(1, slab)
        for dz in (-1, 1):
            flat.append(column(dz, 0, 0))
        for dy in (-1, 1):
            flat.append(row(dy, every, mine, mine, 0))
            for dz in (-1, 1):
                flat.append(corner(dy, dz, mine, pl.ds(0, slab), 0))
        if slide:
            two = pl.ds(1, 2), pl.ds(5, 2)
            for dz in (-1, 1):
                far.append(column(dz, 1, -1))
            for dy in (-1, 1):
                far.append(row(dy, every, *two, -1))
                for dz in (-1, 1):
                    far.append(corner(dy, dz, pl.ds(1, 1), pl.ds(4, 1), -1))
            far.append(
                wires.send(
                    UE.at[level, :, pl.ds(1, 2), pl.ds(TOP, rows)],
                    UE.at[level, :, pl.ds(5, 2), pl.ds(TOP, rows)],
                    -1, 0, 0,
                )
            )
        else:
            for dg, here, there, slot in ((-1, 1, 5, 1), (1, 4, 0, 2)):
                for dz in (-1, 1):
                    far.append(column(dz, slot, dg))
                for dy in (-1, 1):
                    far.append(row(dy, pl.ds(0, 2), pl.ds(here, 1), pl.ds(there, 1), dg))
            for dg, here, there in ((-1, 1, 5), (1, 4, 0)):
                far.append(
                    wires.send(
                        UE.at[level, :, pl.ds(here, 1), pl.ds(TOP, rows)],
                        UE.at[level, :, pl.ds(there, 1), pl.ds(TOP, rows)],
                        dg, 0, 0,
                    )
                )
        return flat, far

    def unpack(level, slots):
        for slot in slots:
            TS[pl.ds(32 * slot, pairs, stride=2), :] = RCU[level, slot, 1]
            TS[pl.ds(32 * slot + 1, pairs, stride=2), :] = RCU[level, slot, 0]
        HT[...] = jnp.transpose(TS[...])

    def pair_lane(f, p):
        if 1 <= p <= slab:
            return 2 * (f * slab + p - 1)
        if p > slab:
            return 32 + 2 * (f * slab + p - 5)
        return 64 + 2 * (f * slab + slab - 1)

    def sides(values, halo_ref, start, at_lane):
        halo = pltpu.roll(halo_ref[pl.ds(start, CHUNK), :], (2 * LANES - at_lane - 1) % LANES, 1)
        behind = jnp.where(lane == 0, halo, pltpu.roll(values, 1, 1))
        ahead = jnp.where(lane == LANES - 1, halo, pltpu.roll(values, LANES - 1, 1))
        return behind, ahead

    def lateral(level, f, p, centre, slope):
        for at, start in chunks:
            values = UE[level, f, p, pl.ds(at, CHUNK), :]
            behind, ahead = sides(values, HT, start, pair_lane(f, p))
            if f == 3:
                PZP[p, pl.ds(start, CHUNK), :] = ahead
                PZM[p, pl.ds(start, CHUNK), :] = behind
            else:
                if slope:
                    ZB[f, p, pl.ds(at, CHUNK), :] = ahead - behind
                if centre:
                    SB[f, p, pl.ds(start, CHUNK), :] = ahead + behind

    def lateral_row(level, f, p, at, corner_at):
        values = UE[level, f, p, pl.ds(at, 1), :]
        left = CE[level, 0, f, p - 1, pl.ds(corner_at, 1), :]
        right = CE[level, 1, f, p - 1, pl.ds(corner_at, 1), :]
        behind = jnp.where(lane_row == 0, pltpu.roll(left, 1, 1), pltpu.roll(values, 1, 1))
        ahead = jnp.where(
            lane_row == LANES - 1,
            pltpu.roll(right, LANES - 1, 1),
            pltpu.roll(values, LANES - 1, 1),
        )
        ZB[f, p, pl.ds(at, 1), :] = ahead - behind

    def sweep(level, base, hbase, offset):
        for p in range(base - 1, base + slab + 1):
            centre = base <= p < base + slab
            lateral(level, 0, p, centre, True)
            lateral(level, 2, p, centre, True)
            if centre:
                lateral(level, 1, p, True, True)
                lateral(level, 3, p, True, False)
                for f in (1, 2):
                    lateral_row(level, f, p, low, TOP - 1)
                    lateral_row(level, f, p, high, TOP)

        @pl.loop(0, slab)
        def _(j):
            p = base + j
            hp = hbase + j
            beyond = g * slab + offset + j >= ng * slab
            for at, start in chunks:
                here = pl.ds(at, CHUNK)
                above, below = pl.ds(at + 1, CHUNK), pl.ds(at - 1, CHUNK)
                flat = pl.ds(start, CHUNK)
                ux, uy, uz = (UE[level, c, p, here, :] for c in range(3))
                pair_x = [UE[level, c, p + 1, here, :] + UE[level, c, p - 1, here, :] for c in range(3)]
                pair_y = [UE[level, c, p, above, :] + UE[level, c, p, below, :] for c in range(3)]
                pair_z = [SB[c, p, flat, :] for c in range(3)]

                def divided_yz(q, hq):
                    return (
                        UE[level, 1, q, above, :] - UE[level, 1, q, below, :]
                        + ZB[2, q, here, :] - HH[hq, here, :]
                    )

                def divided_xz(at_rows):
                    return (
                        UE[level, 0, p + 1, at_rows, :] - UE[level, 0, p - 1, at_rows, :]
                        + ZB[2, p, at_rows, :] - HH[hp, at_rows, :]
                    )

                cross_x = divided_yz(p + 1, hp + 1) - divided_yz(p - 1, hp - 1)
                cross_y = divided_xz(above) - divided_xz(below)
                cross_z = (
                    ZB[0, p + 1, here, :] - ZB[0, p - 1, here, :]
                    + ZB[1, p, above, :] - ZB[1, p, below, :]
                    - GZ[hp, flat, :]
                )
                new_x = 0.12 * ux + 0.28 * pair_x[0] + 0.08 * (pair_y[0] + pair_z[0]) + 0.05 * cross_x
                new_y = 0.12 * uy + 0.28 * pair_y[1] + 0.08 * (pair_x[1] + pair_z[1]) + 0.05 * cross_y
                new_z = 0.12 * uz + 0.28 * pair_z[2] + 0.08 * (pair_x[2] + pair_y[2]) + 0.05 * cross_z
                v = UE[level, 3, p, here, :]
                c = CC[hp, here, :]
                flux = CZP[hp, flat, :] * (PZP[p, flat, :] - v) + CZM[hp, flat, :] * (PZM[p, flat, :] - v)
                for q, hq, r in ((p + 1, hp + 1, here), (p - 1, hp - 1, here), (p, hp, above), (p, hp, below)):
                    flux = flux + (CC[hq, r, :] + c) * (UE[level, 3, q, r, :] - v)
                new_v = v + flux
                if offset:
                    new_x = jnp.where(beyond, 0.0, new_x)
                    new_y = jnp.where(beyond, 0.0, new_y)
                    new_z = jnp.where(beyond, 0.0, new_z)
                    new_v = jnp.where(beyond, 1.0, new_v)
                for f, value in enumerate((new_x, new_y, new_z, new_v)):
                    UE[level + 1, f, 1 + j, here, :] = value

    def h_of(phase):
        return phase * phase * (3.0 - 2.0 * phase)

    def send_phase(step):
        pack([(PH, (step, 1 + p)) for p in range(slab)])
        SCP[step, 1, 0:slab] = TT[pl.ds(0, slab, stride=2), :]
        SCP[step, 0, 0:slab] = TT[pl.ds(1, slab, stride=2), :]
        flat, far = [], []
        slots = ((0, flat, 0), (-1, far, slab)) if step else ((0, flat, 0),)
        for dg, messages, move in slots:
            for dz in (-1, 1):
                messages.append(
                    wires.send(
                        SCP.at[step, 0 if dz < 0 else 1, pl.ds(0, slab)],
                        RCP.at[step, -dg, 1 if dz < 0 else 0, pl.ds(0, slab)],
                        dg, 0, dz,
                    )
                )
            for dy, src, dst in ((-1, TOP, high), (1, TOP + rows - 1, low)):
                messages.append(
                    wires.send(
                        PH.at[step, pl.ds(1, slab), pl.ds(src, 1)],
                        PH.at[step, pl.ds(1 + move, slab), pl.ds(dst, 1)],
                        dg, dy, 0,
                    )
                )
        planes = ((-1, 1, 5, slab), (-2, 1, 9, 1)) if step else ((-1, 1, 5, 1), (1, 4, 0, 1))
        for dg, src, dst, count in planes:
            far.append(
                wires.send(
                    PH.at[step, pl.ds(src, count), pl.ds(TOP, rows)],
                    PH.at[step, pl.ds(dst, count), pl.ds(TOP, rows)],
                    dg, 0, 0,
                )
            )
        return flat, far

    def derive(step, centres, beside):
        slots = (0, 1) if step else (0,)
        for slot in slots:
            TS[pl.ds(8 * slot, slab, stride=2), :] = RCP[step, slot, 1, 0:slab]
            TS[pl.ds(8 * slot + 1, slab, stride=2), :] = RCP[step, slot, 0, 0:slab]
        HT[...] = jnp.transpose(TS[...])
        for p in sorted(centres + beside):
            for at, start in chunks:
                phase = PH[step, p, pl.ds(at, CHUNK), :]
                h = h_of(phase)
                c = 0.0075 + 0.0675 * h
                HH[p, pl.ds(at, CHUNK), :] = 0.52 * h
                CC[p, pl.ds(at, CHUNK), :] = c
                if p in centres:
                    behind, ahead = sides(phase, HT, start, 2 * (p - 1))
                    h_behind, h_ahead = h_of(behind), h_of(ahead)
                    flat = pl.ds(start, CHUNK)
                    GZ[p, flat, :] = 0.52 * (h_ahead - h_behind)
                    CZP[p, flat, :] = c + (0.0075 + 0.0675 * h_ahead)
                    CZM[p, flat, :] = c + (0.0075 + 0.0675 * h_behind)
                    PZ[p, flat, :] = ahead + behind
            if p in centres:
                for at in (low, high):
                    h = h_of(PH[step, p, pl.ds(at, 1), :])
                    HH[p, pl.ds(at, 1), :] = 0.52 * h
                    CC[p, pl.ds(at, 1), :] = 0.0075 + 0.0675 * h

    def phase_update(step, level, base, hbase, offset, store):
        @pl.loop(0, slab)
        def _(j):
            p = base + j
            hp = hbase + j
            beyond = g * slab + offset + j >= ng * slab
            for at, start in chunks:
                here = pl.ds(at, CHUNK)
                above, below = pl.ds(at + 1, CHUNK), pl.ds(at - 1, CHUNK)
                flat = pl.ds(start, CHUNK)
                twice = (
                    UE[level, 0, p + 1, here, :] - UE[level, 0, p - 1, here, :]
                    + UE[level, 1, p, above, :] - UE[level, 1, p, below, :]
                    + ZB[2, p, here, :]
                )
                over = UE[level, 3, p, here, :] - 0.5 + 0.325 * twice - 0.375 * HH[hp, here, :]
                drive = jnp.exp(over) - jnp.exp(-over)
                phase = PH[step, hp, here, :]
                around = (
                    PH[step, hp + 1, here, :] + PH[step, hp - 1, here, :]
                    + PH[step, hp, above, :] + PH[step, hp, below, :]
                    + PZ[hp, flat, :] - 6.0 * phase
                )
                well = phase * (1.0 - phase)
                change = around - well * (2.0 * (1.0 - 2.0 * phase) + 3.0 * drive)
                value = phase + 0.05 * change
                if offset:
                    value = jnp.where(beyond, 0.0, value)
                store(j, at, start, value)

    count = len([p for p in partners if p[0] == 0])
    total = count + sum(
        9 * jnp.where(ok, 1, 0) for ok in (g > 0, g < ng - 1)
    ) + sum(jnp.where(ok, 1, 0) for ok in (g > 1, g < ng - 2))
    pl.semaphore_wait(barrier, total)

    phase_flat, phase_far = send_phase(0)
    flat, far = send_level(0, False)
    wires.receive(phase_flat)
    wires.receive(phase_far)
    derive(0, [1, 2, 3, 4], [0, 5])
    for level in range(3):
        wires.receive(flat)
        wires.receive(far)
        unpack(level, (0, 1, 2))
        sweep(level, 1, 1, 0)
        if level < 2:
            flat, far = send_level(level + 1, False)

    up = [
        wires.send(
            UE.at[3, 0, 4, pl.ds(TOP, rows)],
            UE.at[3, 0, 0, pl.ds(TOP, rows)],
            1, 0, 0,
        )
    ]
    flat, far = send_level(3, True)
    wires.receive(up)
    wires.receive(flat)
    wires.receive(far)
    unpack(3, (0, 1))
    for p in range(1, 5):
        lateral(3, 2, p, False, True)

    def keep(j, at, start, value):
        PH[1, 1 + j, pl.ds(at, CHUNK), :] = value

    phase_update(0, 3, 1, 1, 0, keep)

    phase_flat, phase_far = send_phase(1)
    wires.receive(phase_flat)
    wires.receive(phase_far)
    derive(1, [2, 3, 4, 5, 6, 7, 8], [1, 9])
    for level in (3, 4, 5):
        if level > 3:
            wires.receive(flat)
            wires.receive(far)
        unpack(level, (0, 1))
        sweep(level, 2, level - 1, level - 2)
        if level < 5:
            flat, far = send_level(level + 1, True)

    flat, far = send_level(6, True)
    wires.receive(flat)
    wires.receive(far)
    unpack(6, (0, 1))
    for p in range(2, 6):
        lateral(6, 2, p, False, True)

    def finish(j, at, start, value):
        ph_out[j, pl.ds(start, CHUNK), :] = value

    phase_update(1, 6, 2, 5, 4, finish)
    for p in range(slab):
        pot_out[p] = UE[6, 3, 2 + p, own, :]
        for c in range(3):
            u_out[c, p] = UE[6, c, 2 + p, own, :]
    wires.drain()


def solution(mesh):
    ng, ny, nz = (mesh.shape[a] for a in ("grow", "cy", "cz"))

    def shards(labels, roughness, potential, displacement):
        slab, rows, lanes = labels.shape
        tall = rows + 2 * TOP
        f32 = jnp.float32
        vmem = pl.BlockSpec(memory_space=pltpu.VMEM)
        scratch = [
            (LEVELS, 4, slab + 3, tall, lanes),
            (LEVELS, 2, 3, slab + 1, 16, lanes),
            (LEVELS, 3, 2, 4 * slab, lanes),
            (LEVELS, 2, 4 * slab, lanes),
            (2, 10, tall, lanes),
            (2, 2, 2, 8, lanes),
            (2, 2, 8, lanes),
            (10, tall, lanes),
            (10, tall, lanes),
            (10, rows, lanes),
            (10, rows, lanes),
            (10, rows, lanes),
            (10, rows, lanes),
            (3, slab + 3, tall, lanes),
            (3, slab + 3, rows, lanes),
            (slab + 3, rows, lanes),
            (slab + 3, rows, lanes),
            (lanes, lanes),
            (lanes, lanes),
            (lanes, lanes),
        ]
        return pl.pallas_call(
            functools.partial(kernel, ng, ny, nz),
            out_shape=(
                jax.ShapeDtypeStruct(labels.shape, f32),
                jax.ShapeDtypeStruct(labels.shape, f32),
                jax.ShapeDtypeStruct(displacement.shape, f32),
            ),
            in_specs=[vmem] * 4,
            out_specs=(vmem,) * 3,
            scratch_shapes=[pltpu.VMEM(shape, f32) for shape in scratch]
            + [
                pltpu.SemaphoreType.DMA((COPIES,)),
                pltpu.SemaphoreType.DMA((COPIES,)),
            ],
            compiler_params=pltpu.CompilerParams(
                collective_id=0,
                has_side_effects=True,
                vmem_limit_bytes=60 * 1024 * 1024,
            ),
            name="filament",
        )(labels, roughness, potential, displacement)

    placed = P("grow", "cy", "cz")
    vector = P(None, "grow", "cy", "cz")
    return jax.shard_map(
        shards,
        mesh=mesh,
        in_specs=(placed, placed, placed, vector),
        out_specs=(placed, placed, vector),
        check_vma=False,
    )
```

time: 301 us -> 103 us (0.34)
  the two profiles are of different devices: /device:TPU:3 before, /device:TPU:1 now
where the time goes in v1:
time: 103 us
  Pallas kernels  97.6 us (95%)
  local copies, waits for them, and re-layouts  4.3 us (4%)
    pallas_call x1, Pallas kernels, shards(): pl.pallas_call(functools.partial(kernel, ng, ny, nz), out_shape=(jax.Shap...  97.6 us
    unnamed x5, local copies, waits for them, and re-layouts  4.3 us

profile of v1, /device:TPU:1, one launch (start us, length us, event | category | flops | bytes accessed | tf_op | source)
XLA Modules:
  0.0 102.5 jit_solution(16160056146591931404)
XLA Ops:
  0.6 97.6 %filament.1 = (f32[4,128,128]{2,1,0:T(8,128)}, f32[4,128,128]{2,1,0:T(8,128)}, f32[3,4,128,128]{3,2,1,0:T(8,128)}) custom-call(s32[4,128,128]{2,1,0:T(8,128)} %lab.1, f32[4,128,128]{2,1,0:T(8,128)} %rough.1, f32[4,128,128]{2,1,0:T(8,128)} %pot.1, f32[3,4,128,128]{3,2,1,0:T(8,128)} %disp.1), custom_call_target="tpu_custom_call" | custom-call | tf_op jit(solution)/shard_map/filament/pallas_call | solution.py:517
  98.2 0.0 copy-start
  98.3 1.7 %copy.10 = f32[4,128,128]{2,1,0:T(8,128)} copy(f32[4,128,128]{2,1,0:T(8,128)} %get-tuple-element.6) | data formatting | bytes 524288
  100.0 1.7 %copy.11 = f32[4,128,128]{2,1,0:T(8,128)} copy(f32[4,128,128]{2,1,0:T(8,128)} %get-tuple-element.7) | data formatting | bytes 524288
  101.7 0.0 copy-done
  101.7 0.9 copy.12
Async XLA Ops:
  98.2 3.4 %copy-start = (f32[3,4,128,128]{3,2,1,0:T(8,128)S(1)}, f32[3,4,128,128]{3,2,1,0:T(8,128)}, u32[]{:S(2)}) copy-start(f32[3,4,128,128]{3,2,1,0:T(8,128)} %get-tuple-element.8) | copy-start | bytes 2359300

commit v2 on v1

v2 whole, which is shorter than its diff:
```python
import functools

import jax
import jax.numpy as jnp
from jax import lax
from jax.experimental import pallas as pl
from jax.experimental.pallas import tpu as pltpu
from jax.sharding import PartitionSpec as P

MESH = pl.DeviceIdType.MESH
LANES = 128
TOP = 8
CHUNK = 32
LEVELS = 7
COPIES = 134


class Wires:
    def __init__(self, send_sem, recv_sem, place):
        self.send_sem, self.recv_sem = send_sem, recv_sem
        self.g, self.y, self.z, self.ng, self.ny, self.nz = place
        self.count = 0
        self.pending = []

    def send(self, src, dst, dg, dy, dz):
        index = self.count
        self.count += 1
        target = (
            self.g + dg,
            lax.rem(self.y + dy + self.ny, self.ny),
            lax.rem(self.z + dz + self.nz, self.nz),
        )
        copy = pltpu.make_async_remote_copy(
            src_ref=src,
            dst_ref=dst,
            send_sem=self.send_sem.at[index],
            recv_sem=self.recv_sem.at[index],
            device_id=target,
            device_id_type=MESH,
        )
        self.when_valid(dg, copy.start)
        self.pending.append((dg, copy))
        return (dg, copy)

    def when_valid(self, dg, action):
        if dg == 0:
            action()
        else:
            ok = self.g + dg >= 0 if dg < 0 else self.g + dg < self.ng
            pl.when(ok)(action)

    def receive(self, messages):
        for dg, copy in messages:
            self.when_valid(-dg, copy.wait_recv)

    def drain(self):
        for dg, copy in self.pending:
            self.when_valid(dg, copy.wait_send)


def kernel(
    ng, ny, nz,
    lab, rough, pot, disp,
    out,
    UE, CE, RCU, SCU, PH, RCP, SCP,
    HH, CC, GZ, CZP, CZM, PZ, ZB, SB, PZP, PZM, TS, TT, HT, HP,
    send_sem, recv_sem, load_sem,
):
    g, y, z = lax.axis_index("grow"), lax.axis_index("cy"), lax.axis_index("cz")
    wires = Wires(send_sem, recv_sem, (g, y, z, ng, ny, nz))
    slab = lab.shape[0]
    rows = lab.shape[1]
    low, high = TOP - 1, TOP + rows
    own = pl.ds(TOP, rows)
    pairs = 4 * slab
    f32 = jnp.float32

    barrier = pltpu.get_barrier_semaphore()
    around = [(a, b) for a in (-1, 0, 1) for b in (-1, 0, 1)]
    partners = [(0, a, b) for a, b in around if (a, b) != (0, 0)]
    partners += [(s, a, b) for s in (-1, 1) for a, b in around]
    partners += [(-2, 0, 0), (2, 0, 0)]
    for dg, dy, dz in partners:
        def greet(dg=dg, dy=dy, dz=dz):
            pl.semaphore_signal(
                barrier,
                inc=1,
                device_id=(
                    g + dg,
                    lax.rem(y + dy + ny, ny),
                    lax.rem(z + dz + nz, nz),
                ),
                device_id_type=MESH,
            )
        wires.when_valid(dg, greet)

    loads = [
        pltpu.make_async_copy(
            disp, UE.at[0, pl.ds(0, 3), pl.ds(1, slab), own], load_sem.at[0]
        ),
        pltpu.make_async_copy(pot, UE.at[0, 3, pl.ds(1, slab), own], load_sem.at[1]),
    ]
    for load in loads:
        load.start()
    for p in range(slab):
        mark = lab[p].astype(f32)
        part = 0.3 * rough[p]
        PH[0, 1 + p, own, :] = mark * (1.0 - part) + (1.0 - mark) * part

    plane_shape = UE.shape[3:]

    def pin_outside():
        @pl.when(g == 0)
        def _():
            for level in range(4):
                for f in range(4):
                    UE[level, f, 0] = jnp.zeros(plane_shape, f32)
                RCU[level, 2] = jnp.zeros(RCU.shape[2:], f32)
            PH[0, 0] = jnp.ones(plane_shape, f32)

        @pl.when(g == ng - 1)
        def _():
            is_pot = lax.broadcasted_iota(jnp.int32, (pairs, LANES), 0) % 4 == 3
            for level in range(LEVELS):
                for f in range(4):
                    for p in (5, 6):
                        UE[level, f, p] = jnp.full(plane_shape, 1.0 if f == 3 else 0.0, f32)
                CE[level, :, :, 4] = jnp.zeros((2, 3, 16, LANES), f32)
                for side in range(2):
                    RCU[level, 1, side] = jnp.where(is_pot, 1.0, 0.0)
            PH[0, 5] = jnp.zeros(plane_shape, f32)
            for p in range(5, 10):
                PH[1, p] = jnp.zeros(plane_shape, f32)
            RCP[1, 1] = jnp.zeros(RCP.shape[2:], f32)

        @pl.when(g == ng - 2)
        def _():
            PH[1, 9] = jnp.zeros(plane_shape, f32)

    lane = lax.broadcasted_iota(jnp.int32, (CHUNK, LANES), 1)
    lane_row = lax.broadcasted_iota(jnp.int32, (1, LANES), 1)
    chunks = [(TOP + start, start) for start in range(0, rows, CHUNK)]

    def pack(planes):
        for at, start in chunks:
            tile = None
            for k, ref, index in planes:
                moved = pltpu.roll(ref[index + (pl.ds(at, CHUNK), slice(None))], 2 * k + 1, 1)
                tile = moved if tile is None else jnp.where(lane // 2 == k, moved, tile)
            TS[pl.ds(start, CHUNK), :] = tile
        TT[...] = jnp.transpose(TS[...])

    def pack_level(level, planes):
        pack([(4 * (p - 1) + f, UE, (level, f, p)) for p in planes for f in range(4)])
        for p in planes:
            first = 4 * (p - 1)
            for side in (0, 1):
                SCU[level, side, pl.ds(first, 4)] = TT[pl.ds(2 * first + 1 - side, 4, stride=2), :]

    def row(level, dy, fields, here, there, dg):
        src, dst = (TOP, high) if dy < 0 else (TOP + rows - 1, low)
        return wires.send(
            UE.at[level, fields, here, pl.ds(src, 1)],
            UE.at[level, fields, there, pl.ds(dst, 1)],
            dg, dy, 0,
        )

    def corner(level, dy, dz, here, there, dg):
        src, dst = (TOP, TOP) if dy < 0 else (TOP + rows - 1, TOP - 1)
        return wires.send(
            UE.at[level, pl.ds(0, 3), here, pl.ds(src, 1)],
            CE.at[level, 0 if dz > 0 else 1, :, there, pl.ds(dst, 1)],
            dg, dy, dz,
        )

    def column(level, dz, slot, which, dg):
        return wires.send(
            SCU.at[level, 0 if dz < 0 else 1, which],
            RCU.at[level, slot, 1 if dz < 0 else 0, which],
            dg, 0, dz,
        )

    def planes(level, fields, here, there, dg):
        return wires.send(
            UE.at[level, fields, here, own], UE.at[level, fields, there, own], dg, 0, 0
        )

    every, mine = pl.ds(0, 4), pl.ds(1, slab)

    def send_flat(level, corners=True):
        sent = [column(level, dz, 0, pl.ds(0, pairs), 0) for dz in (-1, 1)]
        for dy in (-1, 1):
            sent.append(row(level, dy, every if corners else pl.ds(1, 1), mine, mine, 0))
            if corners:
                for dz in (-1, 1):
                    sent.append(corner(level, dy, dz, mine, pl.ds(0, slab), 0))
        return sent

    def send_both_ways(level):
        sent = []
        for dg, here, there, slot in ((-1, 1, 5, 1), (1, 4, 0, 2)):
            for dz in (-1, 1):
                sent.append(column(level, dz, slot, pl.ds(4 * (here - 1), 4), dg))
            for dy in (-1, 1):
                sent.append(row(level, dy, pl.ds(0, 2), pl.ds(here, 1), pl.ds(there, 1), dg))
        for dg, here, there in ((-1, 1, 5), (1, 4, 0)):
            sent.append(planes(level, every, pl.ds(here, 1), pl.ds(there, 1), dg))
        return sent

    def send_rims_back(level):
        two = pl.ds(1, 2), pl.ds(5, 2)
        sent = [column(level, dz, 1, pl.ds(0, 8), -1) for dz in (-1, 1)]
        for dy in (-1, 1):
            sent.append(row(level, dy, every, *two, -1))
            for dz in (-1, 1):
                sent.append(corner(level, dy, dz, pl.ds(1, 1), pl.ds(4, 1), -1))
        return sent

    def send_planes_back(level):
        return [planes(level, every, pl.ds(1, 2), pl.ds(5, 2), -1)]

    def unpack(level, slot, count):
        first, size = count
        TS[pl.ds(2 * first, size, stride=2), :] = RCU[level, slot, 1, pl.ds(first, size)]
        TS[pl.ds(2 * first + 1, size, stride=2), :] = RCU[level, slot, 0, pl.ds(first, size)]
        HT[slot] = jnp.transpose(TS[...])

    def halo_lane(f, p):
        if p == 0:
            return 2, 2 * (pairs - 4 + f)
        if p <= slab:
            return 0, 2 * (4 * (p - 1) + f)
        return 1, 2 * (4 * (p - 5) + f)

    def sides(values, halo, at_lane):
        halo = pltpu.roll(halo, (2 * LANES - at_lane - 1) % LANES, 1)
        behind = jnp.where(lane == 0, halo, pltpu.roll(values, 1, 1))
        ahead = jnp.where(lane == LANES - 1, halo, pltpu.roll(values, LANES - 1, 1))
        return behind, ahead

    def lateral(level, f, p, centre):
        slot, at_lane = halo_lane(f, p)
        for at, start in chunks:
            flat = pl.ds(start, CHUNK)
            values = UE[level, f, p, pl.ds(at, CHUNK), :]
            behind, ahead = sides(values, HT[slot, flat, :], at_lane)
            if f == 3:
                PZP[p, flat, :] = ahead
                PZM[p, flat, :] = behind
            else:
                ZB[f, p, pl.ds(at, CHUNK), :] = ahead - behind
                if centre:
                    SB[f, p, flat, :] = ahead + behind

    def lateral_row(level, f, p, at, corner_at):
        values = UE[level, f, p, pl.ds(at, 1), :]
        left = CE[level, 0, f, p - 1, pl.ds(corner_at, 1), :]
        right = CE[level, 1, f, p - 1, pl.ds(corner_at, 1), :]
        behind = jnp.where(lane_row == 0, pltpu.roll(left, 1, 1), pltpu.roll(values, 1, 1))
        ahead = jnp.where(
            lane_row == LANES - 1,
            pltpu.roll(right, LANES - 1, 1),
            pltpu.roll(values, LANES - 1, 1),
        )
        ZB[f, p, pl.ds(at, 1), :] = ahead - behind

    ready = set()

    def once(*key):
        fresh = key not in ready
        ready.add(key)
        return fresh

    def sweep(level, base, hbase, offset, js):
        inside = range(base, base + slab)
        for p in range(min(js) + base - 1, max(js) + base + 2):
            centre = p - base in js
            wanted = (0, 1, 2, 3) if centre else (0, 2)
            if not centre and p - 1 - base not in js and p + 1 - base not in js:
                continue
            for f in wanted:
                if once("side", level, f, p):
                    lateral(level, f, p, p in inside)
            if centre:
                for f in (1, 2):
                    lateral_row(level, f, p, low, TOP - 1)
                    lateral_row(level, f, p, high, TOP)

        @pl.loop(0, len(js))
        def _(i):
            j = js[0] + i * (js[1] - js[0])
            p = base + j
            hp = hbase + j
            beyond = g * slab + offset + j >= ng * slab
            for at, start in chunks:
                here = pl.ds(at, CHUNK)
                above, below = pl.ds(at + 1, CHUNK), pl.ds(at - 1, CHUNK)
                flat = pl.ds(start, CHUNK)
                ux, uy, uz = (UE[level, c, p, here, :] for c in range(3))
                pair_x = [UE[level, c, p + 1, here, :] + UE[level, c, p - 1, here, :] for c in range(3)]
                pair_y = [UE[level, c, p, above, :] + UE[level, c, p, below, :] for c in range(3)]
                pair_z = [SB[c, p, flat, :] for c in range(3)]

                def divided_yz(q, hq):
                    return (
                        UE[level, 1, q, above, :] - UE[level, 1, q, below, :]
                        + ZB[2, q, here, :] - HH[hq, here, :]
                    )

                def divided_xz(at_rows):
                    return (
                        UE[level, 0, p + 1, at_rows, :] - UE[level, 0, p - 1, at_rows, :]
                        + ZB[2, p, at_rows, :] - HH[hp, at_rows, :]
                    )

                cross_x = divided_yz(p + 1, hp + 1) - divided_yz(p - 1, hp - 1)
                cross_y = divided_xz(above) - divided_xz(below)
                cross_z = (
                    ZB[0, p + 1, here, :] - ZB[0, p - 1, here, :]
                    + ZB[1, p, above, :] - ZB[1, p, below, :]
                    - GZ[hp, flat, :]
                )
                new_x = 0.12 * ux + 0.28 * pair_x[0] + 0.08 * (pair_y[0] + pair_z[0]) + 0.05 * cross_x
                new_y = 0.12 * uy + 0.28 * pair_y[1] + 0.08 * (pair_x[1] + pair_z[1]) + 0.05 * cross_y
                new_z = 0.12 * uz + 0.28 * pair_z[2] + 0.08 * (pair_x[2] + pair_y[2]) + 0.05 * cross_z
                v = UE[level, 3, p, here, :]
                c = CC[hp, here, :]
                flux = CZP[hp, flat, :] * (PZP[p, flat, :] - v) + CZM[hp, flat, :] * (PZM[p, flat, :] - v)
                for q, hq, r in ((p + 1, hp + 1, here), (p - 1, hp - 1, here), (p, hp, above), (p, hp, below)):
                    flux = flux + (CC[hq, r, :] + c) * (UE[level, 3, q, r, :] - v)
                new_v = v + flux
                if offset:
                    new_x = jnp.where(beyond, 0.0, new_x)
                    new_y = jnp.where(beyond, 0.0, new_y)
                    new_z = jnp.where(beyond, 0.0, new_z)
                    new_v = jnp.where(beyond, 1.0, new_v)
                for f, value in enumerate((new_x, new_y, new_z, new_v)):
                    UE[level + 1, f, 1 + j, here, :] = value

    def h_of(phase):
        return phase * phase * (3.0 - 2.0 * phase)

    def pack_phase(step):
        pack([(p, PH, (step, 1 + p)) for p in range(slab)])
        SCP[step, 1] = TT[pl.ds(0, slab, stride=2), :]
        SCP[step, 0] = TT[pl.ds(1, slab, stride=2), :]

    def send_phase_rims(step, dg):
        sent = []
        for dz in (-1, 1):
            sent.append(
                wires.send(
                    SCP.at[step, 0 if dz < 0 else 1],
                    RCP.at[step, -dg, 1 if dz < 0 else 0],
                    dg, 0, dz,
                )
            )
        for dy, src, dst in ((-1, TOP, high), (1, TOP + rows - 1, low)):
            sent.append(
                wires.send(
                    PH.at[step, pl.ds(1, slab), pl.ds(src, 1)],
                    PH.at[step, pl.ds(1 - dg * slab, slab), pl.ds(dst, 1)],
                    dg, dy, 0,
                )
            )
        return sent

    def send_phase_planes(step, moves):
        return [
            wires.send(
                PH.at[step, pl.ds(src, count), own], PH.at[step, pl.ds(dst, count), own], dg, 0, 0
            )
            for dg, src, dst, count in moves
        ]

    def unpack_phase(step, slot):
        TS[pl.ds(0, slab, stride=2), :] = RCP[step, slot, 1]
        TS[pl.ds(1, slab, stride=2), :] = RCP[step, slot, 0]
        HP[slot] = jnp.transpose(TS[...])

    def derive(step, p, centre):
        slot = 0 if p <= slab else 1
        for at, start in chunks:
            flat = pl.ds(start, CHUNK)
            phase = PH[step, p, pl.ds(at, CHUNK), :]
            h = h_of(phase)
            c = 0.0075 + 0.0675 * h
            HH[p, pl.ds(at, CHUNK), :] = 0.52 * h
            CC[p, pl.ds(at, CHUNK), :] = c
            if centre:
                behind, ahead = sides(phase, HP[slot, flat, :], 2 * (p - 1 - slot * slab))
                h_behind, h_ahead = h_of(behind), h_of(ahead)
                GZ[p, flat, :] = 0.52 * (h_ahead - h_behind)
                CZP[p, flat, :] = c + (0.0075 + 0.0675 * h_ahead)
                CZM[p, flat, :] = c + (0.0075 + 0.0675 * h_behind)
                PZ[p, flat, :] = ahead + behind
        if centre:
            for at in (low, high):
                h = h_of(PH[step, p, pl.ds(at, 1), :])
                HH[p, pl.ds(at, 1), :] = 0.52 * h
                CC[p, pl.ds(at, 1), :] = 0.0075 + 0.0675 * h

    def phase_update(step, level, base, hbase, offset, js, store):
        for j in js:
            if once("side", level, 2, base + j):
                lateral(level, 2, base + j, True)

        @pl.loop(0, len(js))
        def _(i):
            j = js[0] + i * (js[1] - js[0])
            p = base + j
            hp = hbase + j
            beyond = g * slab + offset + j >= ng * slab
            for at, start in chunks:
                here = pl.ds(at, CHUNK)
                above, below = pl.ds(at + 1, CHUNK), pl.ds(at - 1, CHUNK)
                flat = pl.ds(start, CHUNK)
                twice = (
                    UE[level, 0, p + 1, here, :] - UE[level, 0, p - 1, here, :]
                    + UE[level, 1, p, above, :] - UE[level, 1, p, below, :]
                    + ZB[2, p, here, :]
                )
                over = UE[level, 3, p, here, :] - 0.5 + 0.325 * twice - 0.375 * HH[hp, here, :]
                drive = jnp.exp(over) - jnp.exp(-over)
                phase = PH[step, hp, here, :]
                nearby = (
                    PH[step, hp + 1, here, :] + PH[step, hp - 1, here, :]
                    + PH[step, hp, above, :] + PH[step, hp, below, :]
                    + PZ[hp, flat, :] - 6.0 * phase
                )
                well = phase * (1.0 - phase)
                change = nearby - well * (2.0 * (1.0 - 2.0 * phase) + 3.0 * drive)
                value = phase + 0.05 * change
                if offset:
                    value = jnp.where(beyond, 0.0, value)
                store(j, at, start, value)

    count = len([p for p in partners if p[0] == 0])
    total = count + sum(
        9 * jnp.where(ok, 1, 0) for ok in (g > 0, g < ng - 1)
    ) + sum(jnp.where(ok, 1, 0) for ok in (g > 1, g < ng - 2))
    pack_phase(0)
    for load in loads:
        load.wait()
    pack_level(0, (1, 2, 3, 4))
    pl.semaphore_wait(barrier, total)

    phase_flat = send_phase_rims(0, 0)
    flat = send_flat(0)
    phase_far = send_phase_planes(0, ((-1, 1, 5, 1), (1, 4, 0, 1)))
    far = send_both_ways(0)
    pin_outside()
    wires.receive(phase_flat)
    unpack_phase(0, 0)
    for p in (1, 2, 3, 4):
        derive(0, p, True)
    for level in range(3):
        wires.receive(flat)
        unpack(level, 0, (0, pairs))
        sweep(level, 1, 1, 0, (1, 2))
        pack_level(level + 1, (2, 3))
        if level == 0:
            wires.receive(phase_far)
            derive(0, 0, False)
            derive(0, 5, False)
        wires.receive(far)
        unpack(level, 1, (0, 4))
        unpack(level, 2, (pairs - 4, 4))
        sweep(level, 1, 1, 0, (0, 3))
        pack_level(level + 1, (1, 4))
        flat = send_flat(level + 1)
        if level < 2:
            far = send_both_ways(level + 1)

    ends = [
        planes(3, 0, 4, 0, 1),
        planes(3, 0, 1, 5, -1),
    ]
    far = send_rims_back(3)
    far.append(planes(3, pl.ds(1, 3), pl.ds(1, 2), pl.ds(5, 2), -1))
    far.append(planes(3, 0, 2, 6, -1))
    wires.receive(flat)
    unpack(3, 0, (0, pairs))

    def keep(j, at, start, value):
        PH[1, 1 + j, pl.ds(at, CHUNK), :] = value

    phase_update(0, 3, 1, 1, 0, (1, 2), keep)
    wires.receive(ends)
    phase_update(0, 3, 1, 1, 0, (0, 3), keep)
    pack_phase(1)
    phase_flat = send_phase_rims(1, 0)
    phase_far = send_phase_rims(1, -1)
    phase_far += send_phase_planes(1, ((-1, 1, 5, slab), (-2, 1, 9, 1)))

    wires.receive(phase_flat)
    unpack_phase(1, 0)
    derive(1, 1, False)
    for p in (2, 3, 4):
        derive(1, p, True)
    for level in (3, 4, 5):
        hbase, offset = level - 1, level - 2
        if level > 3:
            wires.receive(flat)
            unpack(level, 0, (0, pairs))
        sweep(level, 2, hbase, offset, (0, 1))
        pack_level(level + 1, (1, 2))
        if level < 5:
            next_far = send_rims_back(level + 1) + send_planes_back(level + 1)
        else:
            next_far = [column(6, dz, 1, pl.ds(0, 4), -1) for dz in (-1, 1)]
            for dy in (-1, 1):
                next_far.append(row(6, dy, pl.ds(1, 1), pl.ds(1, 1), pl.ds(5, 1), -1))
            next_far.append(planes(6, every, 1, 5, -1))
            next_far.append(planes(6, 0, 2, 6, -1))
        if level == 3:
            wires.receive(phase_far)
            unpack_phase(1, 1)
            for p in (5, 6, 7, 8):
                derive(1, p, True)
            derive(1, 9, False)
        wires.receive(far)
        unpack(level, 1, (0, 8))
        sweep(level, 2, hbase, offset, (2, 3))
        pack_level(level + 1, (3, 4))
        flat = send_flat(level + 1, level < 5)
        far = next_far

    def finish(j, at, start, value):
        out[0, j, pl.ds(start, CHUNK), :] = value

    def hand_over(p):
        out[1, p - 2] = UE[6, 3, p, own, :]
        for c in range(3):
            out[2 + c, p - 2] = UE[6, c, p, own, :]

    for p in range(2, 5):
        hand_over(p)
    wires.receive(flat)
    unpack(6, 0, (0, pairs))
    phase_update(1, 6, 2, 5, 4, (0, 1), finish)
    wires.receive(far)
    unpack(6, 1, (0, 4))
    hand_over(5)
    phase_update(1, 6, 2, 5, 4, (2, 3), finish)
    wires.drain()
    assert wires.count == COPIES, wires.count


def deliver(packed, phase, potential, displacement):
    phase[...] = packed[0]
    potential[...] = packed[1]
    for c in range(3):
        displacement[c] = packed[2 + c]


def solution(mesh):
    ng, ny, nz = (mesh.shape[a] for a in ("grow", "cy", "cz"))

    def shards(labels, roughness, potential, displacement):
        slab, rows, lanes = labels.shape
        tall = rows + 2 * TOP
        f32 = jnp.float32
        vmem = pl.BlockSpec(memory_space=pltpu.VMEM)
        anywhere = pl.BlockSpec(memory_space=pl.ANY)
        scratch = [
            (LEVELS, 4, slab + 3, tall, lanes),
            (LEVELS, 2, 3, slab + 1, 16, lanes),
            (LEVELS, 3, 2, 4 * slab, lanes),
            (LEVELS, 2, 4 * slab, lanes),
            (2, 10, tall, lanes),
            (2, 2, 2, slab, lanes),
            (2, 2, slab, lanes),
            (10, tall, lanes),
            (10, tall, lanes),
            (10, rows, lanes),
            (10, rows, lanes),
            (10, rows, lanes),
            (10, rows, lanes),
            (3, slab + 3, tall, lanes),
            (3, slab + 3, rows, lanes),
            (slab + 3, rows, lanes),
            (slab + 3, rows, lanes),
            (lanes, lanes),
            (lanes, lanes),
            (3, lanes, lanes),
            (2, lanes, lanes),
        ]
        packed = pl.pallas_call(
            functools.partial(kernel, ng, ny, nz),
            out_shape=jax.ShapeDtypeStruct((5,) + labels.shape, f32),
            in_specs=[vmem, vmem, anywhere, anywhere],
            out_specs=vmem,
            scratch_shapes=[pltpu.VMEM(shape, f32) for shape in scratch]
            + [
                pltpu.SemaphoreType.DMA((COPIES,)),
                pltpu.SemaphoreType.DMA((COPIES,)),
                pltpu.SemaphoreType.DMA((2,)),
            ],
            compiler_params=pltpu.CompilerParams(
                collective_id=0,
                has_side_effects=True,
                vmem_limit_bytes=40 * 1024 * 1024,
            ),
            name="filament",
        )(labels, roughness, potential, displacement)
        return pl.pallas_call(
            deliver,
            out_shape=(
                jax.ShapeDtypeStruct(labels.shape, f32),
                jax.ShapeDtypeStruct(labels.shape, f32),
                jax.ShapeDtypeStruct(displacement.shape, f32),
            ),
            in_specs=[vmem],
            out_specs=(vmem,) * 3,
            name="deliver",
        )(packed)

    placed = P("grow", "cy", "cz")
    vector = P(None, "grow", "cy", "cz")
    return jax.shard_map(
        shards,
        mesh=mesh,
        in_specs=(placed, placed, placed, vector),
        out_specs=(placed, placed, vector),
        check_vma=False,
    )
```

time: 103 us -> 95.4 us (0.926)
  the two profiles are of different devices: /device:TPU:1 before, /device:TPU:3 now
where the time goes in v2:
time: 95.4 us; the launch traced here: 94.3 us
  Pallas kernels  88.6 us (93%)
  local copies, waits for them, and re-layouts  5.04 us (5%)
    pallas_call x1, Pallas kernels, shards(): pl.pallas_call(functools.partial(kernel, ng, ny, nz), out_shape=jax.Shape...  86.3 us
    unnamed x10, local copies, waits for them, and re-layouts  5.04 us
    pallas_call x1, Pallas kernels, shards(): pl.pallas_call(deliver, out_shape=(jax.ShapeDtypeStruct(labels.shape, f32...  2.38 us

profile of v2, /device:TPU:3, one launch (start us, length us, event | category | flops | bytes accessed | tf_op | source)
XLA Modules:
  0.0 94.3 jit_solution(6308115351093467613)
XLA Ops:
  0.6 0.0 copy-start.1
  0.6 1.1 %copy-done.1 = f32[3,4,128,128]{3,2,1,0:T(8,128)S(1)} copy-done((f32[3,4,128,128]{3,2,1,0:T(8,128)S(1)}, f32[3,4,128,128]{3,2,1,0:T(8,128)}, u32[]{:S(2)}) %copy-start.1) | copy-done | bytes 786456
  1.8 0.0 copy-start.2
  1.8 0.9 %copy-done.2 = s32[4,128,128]{2,1,0:T(8,128)S(1)} copy-done((s32[4,128,128]{2,1,0:T(8,128)S(1)}, s32[4,128,128]{2,1,0:T(8,128)}, u32[]{:S(2)}) %copy-start.2) | copy-done | bytes 262168
  2.7 0.0 copy-start.3
  2.7 0.9 %copy-done.3 = f32[4,128,128]{2,1,0:T(8,128)S(1)} copy-done((f32[4,128,128]{2,1,0:T(8,128)S(1)}, f32[4,128,128]{2,1,0:T(8,128)}, u32[]{:S(2)}) %copy-start.3) | copy-done | bytes 262168
  3.7 0.0 copy-start.4
  3.7 0.9 %copy-done.4 = f32[4,128,128]{2,1,0:T(8,128)S(1)} copy-done((f32[4,128,128]{2,1,0:T(8,128)S(1)}, f32[4,128,128]{2,1,0:T(8,128)}, u32[]{:S(2)}) %copy-start.4) | copy-done | bytes 262168
  4.6 86.3 %filament.1.packed = f32[5,4,128,128]{3,2,1,0:T(8,128)S(1)} custom-call(s32[4,128,128]{2,1,0:T(8,128)S(1)} %copy-done.2, f32[4,128,128]{2,1,0:T(8,128)S(1)} %copy-done.3, f32[4,128,128]{2,1,0:T(8,128)S(1)} %copy-done.4, f32[3,4,128,128]{3,2,1,0:T(8,128)S(1)} %copy-done.1), custom_call_target="tpu_custom_call" | custom-call | tf_op jit(solution)/shard_map/filament/pallas_call | solution.py:589
  90.9 0.0 copy-start
  90.9 1.1 %copy-done = f32[5,4,128,128]{3,2,1,0:T(8,128)} copy-done((f32[5,4,128,128]{3,2,1,0:T(8,128)}, f32[5,4,128,128]{3,2,1,0:T(8,128)S(1)}, u32[]{:S(2)}) %copy-start) | copy-done | bytes 1310744
  92.0 2.4 %deliver.1 = (f32[4,128,128]{2,1,0:T(8,128)}, f32[4,128,128]{2,1,0:T(8,128)}, f32[3,4,128,128]{3,2,1,0:T(8,128)}) custom-call(f32[5,4,128,128]{3,2,1,0:T(8,128)} %copy-done), custom_call_target="tpu_custom_call" | custom-call | tf_op jit(solution)/shard_map/deliver/pallas_call | solution.py:607
Async XLA Ops:
  0.6 1.1 %copy-start.1 = (f32[3,4,128,128]{3,2,1,0:T(8,128)S(1)}, f32[3,4,128,128]{3,2,1,0:T(8,128)}, u32[]{:S(2)}) copy-start(f32[3,4,128,128]{3,2,1,0:T(8,128)} %disp.1) | copy-start | bytes 2359300
  1.8 0.9 %copy-start.2 = (s32[4,128,128]{2,1,0:T(8,128)S(1)}, s32[4,128,128]{2,1,0:T(8,128)}, u32[]{:S(2)}) copy-start(s32[4,128,128]{2,1,0:T(8,128)} %lab.1) | copy-start | bytes 786436
  2.7 0.9 %copy-start.3 = (f32[4,128,128]{2,1,0:T(8,128)S(1)}, f32[4,128,128]{2,1,0:T(8,128)}, u32[]{:S(2)}) copy-start(f32[4,128,128]{2,1,0:T(8,128)} %rough.1) | copy-start | bytes 786436
  3.7 0.9 %copy-start.4 = (f32[4,128,128]{2,1,0:T(8,128)S(1)}, f32[4,128,128]{2,1,0:T(8,128)}, u32[]{:S(2)}) copy-start(f32[4,128,128]{2,1,0:T(8,128)} %pot.1) | copy-start | bytes 786436
  90.9 1.1 %copy-start = (f32[5,4,128,128]{3,2,1,0:T(8,128)}, f32[5,4,128,128]{3,2,1,0:T(8,128)S(1)}, u32[]{:S(2)}) copy-start(f32[5,4,128,128]{3,2,1,0:T(8,128)S(1)} %filament.1.packed) | copy-start | bytes 3932164

commit v3 on v2

--- a/solution.py
+++ b/solution.py
@@ -12,7 +12,7 @@
 TOP = 8
 CHUNK = 32
 LEVELS = 7
-COPIES = 134
+COPIES = 175
 
 
 class Wires:
@@ -64,6 +64,7 @@
     out,
     UE, CE, RCU, SCU, PH, RCP, SCP,
     HH, CC, GZ, CZP, CZM, PZ, ZB, SB, PZP, PZM, TS, TT, HT, HP,
+    LAB, ROU,
     send_sem, recv_sem, load_sem,
 ):
     g, y, z = lax.axis_index("grow"), lax.axis_index("cy"), lax.axis_index("cz")
@@ -99,12 +100,16 @@
             disp, UE.at[0, pl.ds(0, 3), pl.ds(1, slab), own], load_sem.at[0]
         ),
         pltpu.make_async_copy(pot, UE.at[0, 3, pl.ds(1, slab), own], load_sem.at[1]),
+        pltpu.make_async_copy(lab, LAB, load_sem.at[2]),
+        pltpu.make_async_copy(rough, ROU, load_sem.at[3]),
     ]
     for load in loads:
         load.start()
+    loads[2].wait()
+    loads[3].wait()
     for p in range(slab):
-        mark = lab[p].astype(f32)
-        part = 0.3 * rough[p]
+        mark = LAB[p].astype(f32)
+        part = 0.3 * ROU[p]
         PH[0, 1 + p, own, :] = mark * (1.0 - part) + (1.0 - mark) * part
 
     plane_shape = UE.shape[3:]
@@ -120,7 +125,7 @@
 
         @pl.when(g == ng - 1)
         def _():
-            is_pot = lax.broadcasted_iota(jnp.int32, (pairs, LANES), 0) % 4 == 3
+            is_pot = lax.broadcasted_iota(jnp.int32, (pairs, LANES), 0) >= 3 * slab
             for level in range(LEVELS):
                 for f in range(4):
                     for p in (5, 6):
@@ -150,12 +155,19 @@
             TS[pl.ds(start, CHUNK), :] = tile
         TT[...] = jnp.transpose(TS[...])
 
-    def pack_level(level, planes):
-        pack([(4 * (p - 1) + f, UE, (level, f, p)) for p in planes for f in range(4)])
-        for p in planes:
-            first = 4 * (p - 1)
-            for side in (0, 1):
-                SCU[level, side, pl.ds(first, 4)] = TT[pl.ds(2 * first + 1 - side, 4, stride=2), :]
+    def pair(f, q):
+        return 3 * slab + q - 1 if f == 3 else 3 * (q - 1) + f
+
+    def pack_level(level, planes, fields=(0, 1, 2, 3)):
+        pack([(pair(f, q), UE, (level, f, q)) for q in planes for f in fields])
+        for q in planes:
+            for f in fields:
+                if f in (0, 3):
+                    first, size = pair(f, q), 1 if f == 3 else 3
+                    for side in (0, 1):
+                        SCU[level, side, pl.ds(first, size)] = TT[
+                            pl.ds(2 * first + 1 - side, size, stride=2), :
+                        ]
 
     def row(level, dy, fields, here, there, dg):
         src, dst = (TOP, high) if dy < 0 else (TOP + rows - 1, low)
@@ -186,51 +198,55 @@
         )
 
     every, mine = pl.ds(0, 4), pl.ds(1, slab)
-
-    def send_flat(level, corners=True):
-        sent = [column(level, dz, 0, pl.ds(0, pairs), 0) for dz in (-1, 1)]
+    u_fields, v_field = pl.ds(0, 3), pl.ds(3, 1)
+    u_pairs, v_pairs = pl.ds(0, 3 * slab), pl.ds(3 * slab, slab)
+
+    def send_flat_u(level):
+        sent = [column(level, dz, 0, u_pairs, 0) for dz in (-1, 1)]
         for dy in (-1, 1):
-            sent.append(row(level, dy, every if corners else pl.ds(1, 1), mine, mine, 0))
-            if corners:
-                for dz in (-1, 1):
-                    sent.append(corner(level, dy, dz, mine, pl.ds(0, slab), 0))
+            sent.append(row(level, dy, u_fields, mine, mine, 0))
+            for dz in (-1, 1):
+                sent.append(corner(level, dy, dz, mine, pl.ds(0, slab), 0))
         return sent
 
-    def send_both_ways(level):
+    def send_flat_v(level):
+        sent = [column(level, dz, 0, v_pairs, 0) for dz in (-1, 1)]
+        return sent + [row(level, dy, v_field, mine, mine, 0) for dy in (-1, 1)]
+
+    def send_both_ways_u(level):
         sent = []
         for dg, here, there, slot in ((-1, 1, 5, 1), (1, 4, 0, 2)):
             for dz in (-1, 1):
-                sent.append(column(level, dz, slot, pl.ds(4 * (here - 1), 4), dg))
+                sent.append(column(level, dz, slot, pl.ds(3 * (here - 1), 3), dg))
             for dy in (-1, 1):
                 sent.append(row(level, dy, pl.ds(0, 2), pl.ds(here, 1), pl.ds(there, 1), dg))
         for dg, here, there in ((-1, 1, 5), (1, 4, 0)):
-            sent.append(planes(level, every, pl.ds(here, 1), pl.ds(there, 1), dg))
+            sent.append(planes(level, u_fields, here, there, dg))
         return sent
+
+    def send_both_ways_v(level):
+        return [planes(level, 3, here, there, dg) for dg, here, there in ((-1, 1, 5), (1, 4, 0))]
 
     def send_rims_back(level):
         two = pl.ds(1, 2), pl.ds(5, 2)
-        sent = [column(level, dz, 1, pl.ds(0, 8), -1) for dz in (-1, 1)]
+        sent = []
+        for dz in (-1, 1):
+            sent.append(column(level, dz, 1, pl.ds(0, 6), -1))
+            sent.append(column(level, dz, 1, pl.ds(3 * slab, 2), -1))
         for dy in (-1, 1):
             sent.append(row(level, dy, every, *two, -1))
             for dz in (-1, 1):
                 sent.append(corner(level, dy, dz, pl.ds(1, 1), pl.ds(4, 1), -1))
         return sent
 
-    def send_planes_back(level):
-        return [planes(level, every, pl.ds(1, 2), pl.ds(5, 2), -1)]
-
-    def unpack(level, slot, count):
-        first, size = count
+    def unpack(level, slot, first, size):
         TS[pl.ds(2 * first, size, stride=2), :] = RCU[level, slot, 1, pl.ds(first, size)]
         TS[pl.ds(2 * first + 1, size, stride=2), :] = RCU[level, slot, 0, pl.ds(first, size)]
-        HT[slot] = jnp.transpose(TS[...])
+        HT[slot if first < 3 * slab else 3 + slot] = jnp.transpose(TS[...])
 
     def halo_lane(f, p):
-        if p == 0:
-            return 2, 2 * (pairs - 4 + f)
-        if p <= slab:
-            return 0, 2 * (4 * (p - 1) + f)
-        return 1, 2 * (4 * (p - 5) + f)
+        slot, q = (2, slab) if p == 0 else (0, p) if p <= slab else (1, p - slab)
+        return slot + (3 if f == 3 else 0), 2 * pair(f, q)
 
     def sides(values, halo, at_lane):
         halo = pltpu.roll(halo, (2 * LANES - at_lane - 1) % LANES, 1)
@@ -271,17 +287,18 @@
         ready.add(key)
         return fresh
 
-    def sweep(level, base, hbase, offset, js):
+    def sweep(level, base, hbase, offset, js, displace=True, relax=True):
         inside = range(base, base + slab)
         for p in range(min(js) + base - 1, max(js) + base + 2):
             centre = p - base in js
-            wanted = (0, 1, 2, 3) if centre else (0, 2)
+            wanted = (0, 1, 2) if centre else (0, 2)
+            wanted = (wanted if displace else ()) + ((3,) if relax and centre else ())
             if not centre and p - 1 - base not in js and p + 1 - base not in js:
                 continue
             for f in wanted:
                 if once("side", level, f, p):
                     lateral(level, f, p, p in inside)
-            if centre:
+            if centre and displace:
                 for f in (1, 2):
                     lateral_row(level, f, p, low, TOP - 1)
                     lateral_row(level, f, p, high, TOP)
@@ -296,46 +313,48 @@
                 here = pl.ds(at, CHUNK)
                 above, below = pl.ds(at + 1, CHUNK), pl.ds(at - 1, CHUNK)
                 flat = pl.ds(start, CHUNK)
-                ux, uy, uz = (UE[level, c, p, here, :] for c in range(3))
-                pair_x = [UE[level, c, p + 1, here, :] + UE[level, c, p - 1, here, :] for c in range(3)]
-                pair_y = [UE[level, c, p, above, :] + UE[level, c, p, below, :] for c in range(3)]
-                pair_z = [SB[c, p, flat, :] for c in range(3)]
-
-                def divided_yz(q, hq):
-                    return (
-                        UE[level, 1, q, above, :] - UE[level, 1, q, below, :]
-                        + ZB[2, q, here, :] - HH[hq, here, :]
+                if displace:
+                    ux, uy, uz = (UE[level, c, p, here, :] for c in range(3))
+                    pair_x = [UE[level, c, p + 1, here, :] + UE[level, c, p - 1, here, :] for c in range(3)]
+                    pair_y = [UE[level, c, p, above, :] + UE[level, c, p, below, :] for c in range(3)]
+                    pair_z = [SB[c, p, flat, :] for c in range(3)]
+
+                    def divided_yz(q, hq):
+                        return (
+                            UE[level, 1, q, above, :] - UE[level, 1, q, below, :]
+                            + ZB[2, q, here, :] - HH[hq, here, :]
+                        )
+
+                    def divided_xz(at_rows):
+                        return (
+                            UE[level, 0, p + 1, at_rows, :] - UE[level, 0, p - 1, at_rows, :]
+                            + ZB[2, p, at_rows, :] - HH[hp, at_rows, :]
+                        )
+
+                    cross_x = divided_yz(p + 1, hp + 1) - divided_yz(p - 1, hp - 1)
+                    cross_y = divided_xz(above) - divided_xz(below)
+                    cross_z = (
+                        ZB[0, p + 1, here, :] - ZB[0, p - 1, here, :]
+                        + ZB[1, p, above, :] - ZB[1, p, below, :]
+                        - GZ[hp, flat, :]
                     )
-
-                def divided_xz(at_rows):
-                    return (
-                        UE[level, 0, p + 1, at_rows, :] - UE[level, 0, p - 1, at_rows, :]
-                        + ZB[2, p, at_rows, :] - HH[hp, at_rows, :]
-                    )
-
-                cross_x = divided_yz(p + 1, hp + 1) - divided_yz(p - 1, hp - 1)
-                cross_y = divided_xz(above) - divided_xz(below)
-                cross_z = (
-                    ZB[0, p + 1, here, :] - ZB[0, p - 1, here, :]
-                    + ZB[1, p, above, :] - ZB[1, p, below, :]
-                    - GZ[hp, flat, :]
-                )
-                new_x = 0.12 * ux + 0.28 * pair_x[0] + 0.08 * (pair_y[0] + pair_z[0]) + 0.05 * cross_x
-                new_y = 0.12 * uy + 0.28 * pair_y[1] + 0.08 * (pair_x[1] + pair_z[1]) + 0.05 * cross_y
-                new_z = 0.12 * uz + 0.28 * pair_z[2] + 0.08 * (pair_x[2] + pair_y[2]) + 0.05 * cross_z
-                v = UE[level, 3, p, here, :]
-                c = CC[hp, here, :]
-                flux = CZP[hp, flat, :] * (PZP[p, flat, :] - v) + CZM[hp, flat, :] * (PZM[p, flat, :] - v)
-                for q, hq, r in ((p + 1, hp + 1, here), (p - 1, hp - 1, here), (p, hp, above), (p, hp, below)):
-                    flux = flux + (CC[hq, r, :] + c) * (UE[level, 3, q, r, :] - v)
-                new_v = v + flux
-                if offset:
-                    new_x = jnp.where(beyond, 0.0, new_x)
-                    new_y = jnp.where(beyond, 0.0, new_y)
-                    new_z = jnp.where(beyond, 0.0, new_z)
-                    new_v = jnp.where(beyond, 1.0, new_v)
-                for f, value in enumerate((new_x, new_y, new_z, new_v)):
-                    UE[level + 1, f, 1 + j, here, :] = value
+                    new_x = 0.12 * ux + 0.28 * pair_x[0] + 0.08 * (pair_y[0] + pair_z[0]) + 0.05 * cross_x
+                    new_y = 0.12 * uy + 0.28 * pair_y[1] + 0.08 * (pair_x[1] + pair_z[1]) + 0.05 * cross_y
+                    new_z = 0.12 * uz + 0.28 * pair_z[2] + 0.08 * (pair_x[2] + pair_y[2]) + 0.05 * cross_z
+                    for f, value in enumerate((new_x, new_y, new_z)):
+                        if offset:
+                            value = jnp.where(beyond, 0.0, value)
+                        UE[level + 1, f, 1 + j, here, :] = value
+                if relax:
+                    v = UE[level, 3, p, here, :]
+                    c = CC[hp, here, :]
+                    flux = CZP[hp, flat, :] * (PZP[p, flat, :] - v) + CZM[hp, flat, :] * (PZM[p, flat, :] - v)
+                    for q, hq, r in ((p + 1, hp + 1, here), (p - 1, hp - 1, here), (p, hp, above), (p, hp, below)):
+                        flux = flux + (CC[hq, r, :] + c) * (UE[level, 3, q, r, :] - v)
+                    new_v = v + flux
+                    if offset:
+                        new_v = jnp.where(beyond, 1.0, new_v)
+                    UE[level + 1, 3, 1 + j, here, :] = new_v
 
     def h_of(phase):
         return phase * phase * (3.0 - 2.0 * phase)
@@ -440,47 +459,56 @@
         9 * jnp.where(ok, 1, 0) for ok in (g > 0, g < ng - 1)
     ) + sum(jnp.where(ok, 1, 0) for ok in (g > 1, g < ng - 2))
     pack_phase(0)
-    for load in loads:
-        load.wait()
+    loads[0].wait()
+    loads[1].wait()
     pack_level(0, (1, 2, 3, 4))
     pl.semaphore_wait(barrier, total)
 
     phase_flat = send_phase_rims(0, 0)
-    flat = send_flat(0)
+    flat_u = send_flat_u(0)
+    flat_v = send_flat_v(0)
+    far_u = send_both_ways_u(0)
     phase_far = send_phase_planes(0, ((-1, 1, 5, 1), (1, 4, 0, 1)))
-    far = send_both_ways(0)
+    far_v = send_both_ways_v(0)
     pin_outside()
     wires.receive(phase_flat)
     unpack_phase(0, 0)
     for p in (1, 2, 3, 4):
         derive(0, p, True)
     for level in range(3):
-        wires.receive(flat)
-        unpack(level, 0, (0, pairs))
-        sweep(level, 1, 1, 0, (1, 2))
-        pack_level(level + 1, (2, 3))
+        wires.receive(flat_u)
+        unpack(level, 0, 0, 3 * slab)
+        sweep(level, 1, 1, 0, (1, 2), relax=False)
+        pack_level(level + 1, (2, 3), (0, 1, 2))
+        wires.receive(flat_v)
+        unpack(level, 0, 3 * slab, slab)
+        sweep(level, 1, 1, 0, (1, 2), displace=False)
+        pack_level(level + 1, (2, 3), (3,))
+        wires.receive(far_u)
         if level == 0:
             wires.receive(phase_far)
             derive(0, 0, False)
             derive(0, 5, False)
-        wires.receive(far)
-        unpack(level, 1, (0, 4))
-        unpack(level, 2, (pairs - 4, 4))
-        sweep(level, 1, 1, 0, (0, 3))
-        pack_level(level + 1, (1, 4))
-        flat = send_flat(level + 1)
+        unpack(level, 1, 0, 3)
+        unpack(level, 2, 3 * (slab - 1), 3)
+        sweep(level, 1, 1, 0, (0, 3), relax=False)
+        pack_level(level + 1, (1, 4), (0, 1, 2))
+        flat_u = send_flat_u(level + 1)
         if level < 2:
-            far = send_both_ways(level + 1)
-
-    ends = [
-        planes(3, 0, 4, 0, 1),
-        planes(3, 0, 1, 5, -1),
-    ]
+            far_u = send_both_ways_u(level + 1)
+        else:
+            ends = [planes(3, 0, 4, 0, 1), planes(3, 0, 1, 5, -1)]
+        wires.receive(far_v)
+        sweep(level, 1, 1, 0, (0, 3), displace=False)
+        pack_level(level + 1, (1, 4), (3,))
+        flat_v = send_flat_v(level + 1)
+        if level < 2:
+            far_v = send_both_ways_v(level + 1)
+
     far = send_rims_back(3)
-    far.append(planes(3, pl.ds(1, 3), pl.ds(1, 2), pl.ds(5, 2), -1))
-    far.append(planes(3, 0, 2, 6, -1))
-    wires.receive(flat)
-    unpack(3, 0, (0, pairs))
+    far.append(planes(3, pl.ds(1, 3), 1, 5, -1))
+    wires.receive(flat_u)
+    unpack(3, 0, 0, 3 * slab)
 
     def keep(j, at, start, value):
         PH[1, 1 + j, pl.ds(at, CHUNK), :] = value
@@ -491,8 +519,12 @@
     pack_phase(1)
     phase_flat = send_phase_rims(1, 0)
     phase_far = send_phase_rims(1, -1)
-    phase_far += send_phase_planes(1, ((-1, 1, 5, slab), (-2, 1, 9, 1)))
-
+    phase_far += send_phase_planes(1, ((-1, 1, 5, 2),))
+    far.append(planes(3, every, 2, 6, -1))
+    phase_later = send_phase_planes(1, ((-1, 3, 7, 2), (-2, 1, 9, 1)))
+
+    wires.receive(flat_v)
+    unpack(3, 0, 3 * slab, slab)
     wires.receive(phase_flat)
     unpack_phase(1, 0)
     derive(1, 1, False)
@@ -502,28 +534,42 @@
         hbase, offset = level - 1, level - 2
         if level > 3:
             wires.receive(flat)
-            unpack(level, 0, (0, pairs))
+            unpack(level, 0, 0, 3 * slab)
+            unpack(level, 0, 3 * slab, slab)
         sweep(level, 2, hbase, offset, (0, 1))
         pack_level(level + 1, (1, 2))
         if level < 5:
-            next_far = send_rims_back(level + 1) + send_planes_back(level + 1)
+            next_far = send_rims_back(level + 1)
+            next_far.append(planes(level + 1, every, 1, 5, -1))
+            next_far.append(planes(level + 1, 0, 2, 6, -1))
         else:
-            next_far = [column(6, dz, 1, pl.ds(0, 4), -1) for dz in (-1, 1)]
+            next_far = [column(6, dz, 1, pl.ds(0, 3), -1) for dz in (-1, 1)]
             for dy in (-1, 1):
                 next_far.append(row(6, dy, pl.ds(1, 1), pl.ds(1, 1), pl.ds(5, 1), -1))
             next_far.append(planes(6, every, 1, 5, -1))
-            next_far.append(planes(6, 0, 2, 6, -1))
         if level == 3:
             wires.receive(phase_far)
             unpack_phase(1, 1)
-            for p in (5, 6, 7, 8):
-                derive(1, p, True)
-            derive(1, 9, False)
+            derive(1, 5, True)
+            derive(1, 6, True)
+        elif level == 4:
+            wires.receive(phase_later)
+            derive(1, 7, True)
         wires.receive(far)
-        unpack(level, 1, (0, 8))
+        unpack(level, 1, 0, 6)
+        unpack(level, 1, 3 * slab, 2)
+        if level == 5:
+            derive(1, 8, True)
         sweep(level, 2, hbase, offset, (2, 3))
-        pack_level(level + 1, (3, 4))
-        flat = send_flat(level + 1, level < 5)
+        if level < 5:
+            pack_level(level + 1, (3, 4))
+            flat = send_flat_u(level + 1) + send_flat_v(level + 1)
+            next_far.append(planes(level + 1, pl.ds(1, 3), 2, 6, -1))
+        else:
+            pack_level(6, (3, 4), (0, 1, 2))
+            flat = [column(6, dz, 0, u_pairs, 0) for dz in (-1, 1)]
+            flat += [row(6, dy, pl.ds(1, 1), mine, mine, 0) for dy in (-1, 1)]
+            next_far.append(planes(6, 0, 2, 6, -1))
         far = next_far
 
     def finish(j, at, start, value):
@@ -537,21 +583,26 @@
     for p in range(2, 5):
         hand_over(p)
     wires.receive(flat)
-    unpack(6, 0, (0, pairs))
+    unpack(6, 0, 0, 3 * slab)
     phase_update(1, 6, 2, 5, 4, (0, 1), finish)
     wires.receive(far)
-    unpack(6, 1, (0, 4))
+    unpack(6, 1, 0, 3)
     hand_over(5)
     phase_update(1, 6, 2, 5, 4, (2, 3), finish)
     wires.drain()
     assert wires.count == COPIES, wires.count
 
 
-def deliver(packed, phase, potential, displacement):
-    phase[...] = packed[0]
-    potential[...] = packed[1]
-    for c in range(3):
-        displacement[c] = packed[2 + c]
+def deliver(packed, phase, potential, displacement, sem):
+    copies = [
+        pltpu.make_async_copy(packed.at[0], phase, sem.at[0]),
+        pltpu.make_async_copy(packed.at[1], potential, sem.at[1]),
+        pltpu.make_async_copy(packed.at[pl.ds(2, 3)], displacement, sem.at[2]),
+    ]
+    for copy in copies:
+        copy.start()
+    for copy in copies:
+        copy.wait()
 
 
 def solution(mesh):
@@ -562,7 +613,7 @@
         tall = rows + 2 * TOP
         f32 = jnp.float32
         vmem = pl.BlockSpec(memory_space=pltpu.VMEM)
-        anywhere = pl.BlockSpec(memory_space=pl.ANY)
+        hbm = pl.BlockSpec(memory_space=pltpu.HBM)
         scratch = [
             (LEVELS, 4, slab + 3, tall, lanes),
             (LEVELS, 2, 3, slab + 1, 16, lanes),
@@ -583,19 +634,21 @@
             (slab + 3, rows, lanes),
             (lanes, lanes),
             (lanes, lanes),
-            (3, lanes, lanes),
+            (5, lanes, lanes),
             (2, lanes, lanes),
         ]
         packed = pl.pallas_call(
             functools.partial(kernel, ng, ny, nz),
             out_shape=jax.ShapeDtypeStruct((5,) + labels.shape, f32),
-            in_specs=[vmem, vmem, anywhere, anywhere],
+            in_specs=[hbm] * 4,
             out_specs=vmem,
             scratch_shapes=[pltpu.VMEM(shape, f32) for shape in scratch]
             + [
+                pltpu.VMEM(labels.shape, jnp.int32),
+                pltpu.VMEM(labels.shape, f32),
                 pltpu.SemaphoreType.DMA((COPIES,)),
                 pltpu.SemaphoreType.DMA((COPIES,)),
-                pltpu.SemaphoreType.DMA((2,)),
+                pltpu.SemaphoreType.DMA((4,)),
             ],
             compiler_params=pltpu.CompilerParams(
                 collective_id=0,
@@ -603,7 +656,7 @@
                 vmem_limit_bytes=40 * 1024 * 1024,
             ),
             name="filament",
-        )(labels, roughness, potential, displacement)
+        )(*(pltpu.with_memory_space_constraint(a, pltpu.HBM) for a in (labels, roughness, potential, displacement)))
         return pl.pallas_call(
             deliver,
             out_shape=(
@@ -611,8 +664,10 @@
                 jax.ShapeDtypeStruct(labels.shape, f32),
                 jax.ShapeDtypeStruct(displacement.shape, f32),
             ),
-            in_specs=[vmem],
-            out_specs=(vmem,) * 3,
+            in_specs=[pl.BlockSpec(memory_space=pl.ANY)],
+            out_specs=(hbm,) * 3,
+            scratch_shapes=[pltpu.SemaphoreType.DMA((3,))],
+            compiler_params=pltpu.CompilerParams(vmem_limit_bytes=4 * 1024 * 1024),
             name="deliver",
         )(packed)
 

time: 95.4 us -> 84.4 us (0.88)
  Pallas kernels: 88.6 us -> 83.4 us
  local copies, waits for them, and re-layouts: 5.04 us -> 0 us
    unnamed x10 -> x0, local copies, waits for them, and re-layouts: 5.04 us -> none
    pallas_call x1, Pallas kernels: 86.3 us -> 82.3 us  [shards(): pl.pallas_call(functools.partial(kernel, ng, ny, nz), out_shape=jax.Shape...]
    pallas_call x1, Pallas kernels: 2.38 us -> 1.08 us  [shards(): pl.pallas_call(deliver, out_shape=(jax.ShapeDtypeStruct(labels.shape, f32...]
where the time goes in v3:
time: 84.4 us; the launch traced here: 84.2 us
  Pallas kernels  83.4 us (99%)
    pallas_call x1, Pallas kernels, shards(): pl.pallas_call(functools.partial(kernel, ng, ny, nz), out_shape=jax.Shape...  82.3 us

profile of v3, /device:TPU:3, one launch (start us, length us, event | category | flops | bytes accessed | tf_op | source)
XLA Modules:
  0.0 84.2 jit_solution(11662956697371844492)
XLA Ops:
  0.6 82.3 %filament.1.packed = f32[5,4,128,128]{3,2,1,0:T(8,128)S(1)} custom-call(s32[4,128,128]{2,1,0:T(8,128)} %lab.1, f32[4,128,128]{2,1,0:T(8,128)} %rough.1, f32[4,128,128]{2,1,0:T(8,128)} %pot.1, f32[3,4,128,128]{3,2,1,0:T(8,128)} %disp.1), custom_call_target="tpu_custom_call" | custom-call | tf_op jit(solution)/shard_map/filament/pallas_call | solution.py:640
  82.9 1.1 %deliver.1 = (f32[4,128,128]{2,1,0:T(8,128)}, f32[4,128,128]{2,1,0:T(8,128)}, f32[3,4,128,128]{3,2,1,0:T(8,128)}) custom-call(f32[5,4,128,128]{3,2,1,0:T(8,128)S(1)} %filament.1.packed), custom_call_target="tpu_custom_call" | custom-call | tf_op jit(solution)/shard_map/deliver/pallas_call | solution.py:660

commit v4 on v3

--- a/solution.py
+++ b/solution.py
@@ -280,6 +280,11 @@
         )
         ZB[f, p, pl.ds(at, 1), :] = ahead - behind
 
+    def each(js):
+        if len(js) == 1:
+            return lambda body: body(js[0])
+        return lambda body: pl.loop(0, len(js))(lambda i: body(js[0] + i * (js[1] - js[0])))
+
     ready = set()
 
     def once(*key):
@@ -303,9 +308,8 @@
                     lateral_row(level, f, p, low, TOP - 1)
                     lateral_row(level, f, p, high, TOP)
 
-        @pl.loop(0, len(js))
-        def _(i):
-            j = js[0] + i * (js[1] - js[0])
+        @each(js)
+        def _(j):
             p = base + j
             hp = hbase + j
             beyond = g * slab + offset + j >= ng * slab
@@ -424,9 +428,8 @@
             if once("side", level, 2, base + j):
                 lateral(level, 2, base + j, True)
 
-        @pl.loop(0, len(js))
-        def _(i):
-            j = js[0] + i * (js[1] - js[0])
+        @each(js)
+        def _(j):
             p = base + j
             hp = hbase + j
             beyond = g * slab + offset + j >= ng * slab
@@ -480,27 +483,35 @@
         unpack(level, 0, 0, 3 * slab)
         sweep(level, 1, 1, 0, (1, 2), relax=False)
         pack_level(level + 1, (2, 3), (0, 1, 2))
-        wires.receive(flat_v)
-        unpack(level, 0, 3 * slab, slab)
-        sweep(level, 1, 1, 0, (1, 2), displace=False)
-        pack_level(level + 1, (2, 3), (3,))
-        wires.receive(far_u)
-        if level == 0:
-            wires.receive(phase_far)
-            derive(0, 0, False)
-            derive(0, 5, False)
-        unpack(level, 1, 0, 3)
-        unpack(level, 2, 3 * (slab - 1), 3)
-        sweep(level, 1, 1, 0, (0, 3), relax=False)
+        seen = set(ready)
+        for core in (0, 1):
+
+            @pl.when(lax.rem(g, 2) == core)
+            def _(core=core):
+                ready.clear()
+                ready.update(seen)
+                for right in (True, False) if core == 0 else (False, True):
+                    wires.receive([m for m in far_u if (m[0] < 0) == right])
+                    if level == 0:
+                        wires.receive([m for m in phase_far if (m[0] < 0) == right])
+                        derive(0, 5 if right else 0, False)
+                    if right:
+                        unpack(level, 1, 0, 3)
+                    else:
+                        unpack(level, 2, 3 * (slab - 1), 3)
+                    sweep(level, 1, 1, 0, (3,) if right else (0,), relax=False)
+
         pack_level(level + 1, (1, 4), (0, 1, 2))
         flat_u = send_flat_u(level + 1)
         if level < 2:
             far_u = send_both_ways_u(level + 1)
         else:
             ends = [planes(3, 0, 4, 0, 1), planes(3, 0, 1, 5, -1)]
+        wires.receive(flat_v)
         wires.receive(far_v)
-        sweep(level, 1, 1, 0, (0, 3), displace=False)
-        pack_level(level + 1, (1, 4), (3,))
+        unpack(level, 0, 3 * slab, slab)
+        sweep(level, 1, 1, 0, (0, 1, 2, 3), displace=False)
+        pack_level(level + 1, (1, 2, 3, 4), (3,))
         flat_v = send_flat_v(level + 1)
         if level < 2:
             far_v = send_both_ways_v(level + 1)

time: 84.4 us -> 80.4 us (0.953)
  Pallas kernels: 83.4 us -> 79 us
    pallas_call x1, Pallas kernels: 82.3 us -> 77.9 us  [shards(): pl.pallas_call(functools.partial(kernel, ng, ny, nz), out_shape=jax.Shape...]
where the time goes in v4:
time: 80.4 us; the launch traced here: 79.8 us
  Pallas kernels  79 us (98%)
    pallas_call x1, Pallas kernels, shards(): pl.pallas_call(functools.partial(kernel, ng, ny, nz), out_shape=jax.Shape...  77.9 us

profile of v4, /device:TPU:3, one launch (start us, length us, event | category | flops | bytes accessed | tf_op | source)
XLA Modules:
  0.0 79.8 jit_solution(1788706630556640430)
XLA Ops:
  0.6 77.9 %filament.1.packed = f32[5,4,128,128]{3,2,1,0:T(8,128)S(1)} custom-call(s32[4,128,128]{2,1,0:T(8,128)} %lab.1, f32[4,128,128]{2,1,0:T(8,128)} %rough.1, f32[4,128,128]{2,1,0:T(8,128)} %pot.1, f32[3,4,128,128]{3,2,1,0:T(8,128)} %disp.1), custom_call_target="tpu_custom_call" | custom-call | tf_op jit(solution)/shard_map/filament/pallas_call | solution.py:651
  78.5 1.1 %deliver.1 = (f32[4,128,128]{2,1,0:T(8,128)}, f32[4,128,128]{2,1,0:T(8,128)}, f32[3,4,128,128]{3,2,1,0:T(8,128)}) custom-call(f32[5,4,128,128]{3,2,1,0:T(8,128)S(1)} %filament.1.packed), custom_call_target="tpu_custom_call" | custom-call | tf_op jit(solution)/shard_map/deliver/pallas_call | solution.py:671

commit v5 on v4

--- a/solution.py
+++ b/solution.py
@@ -12,7 +12,7 @@
 TOP = 8
 CHUNK = 32
 LEVELS = 7
-COPIES = 175
+COPIES = 173
 
 
 class Wires:
@@ -40,7 +40,7 @@
         )
         self.when_valid(dg, copy.start)
         self.pending.append((dg, copy))
-        return (dg, copy)
+        return (dg, copy, dy != 0)
 
     def when_valid(self, dg, action):
         if dg == 0:
@@ -50,7 +50,7 @@
             pl.when(ok)(action)
 
     def receive(self, messages):
-        for dg, copy in messages:
+        for dg, copy, _ in messages:
             self.when_valid(-dg, copy.wait_recv)
 
     def drain(self):
@@ -177,6 +177,12 @@
             dg, dy, 0,
         )
 
+    def straight(messages):
+        return [m for m in messages if not m[2]]
+
+    def across(messages):
+        return [m for m in messages if m[2]]
+
     def corner(level, dy, dz, here, there, dg):
         src, dst = (TOP, TOP) if dy < 0 else (TOP + rows - 1, TOP - 1)
         return wires.send(
@@ -244,9 +250,16 @@
         TS[pl.ds(2 * first + 1, size, stride=2), :] = RCU[level, slot, 0, pl.ds(first, size)]
         HT[slot if first < 3 * slab else 3 + slot] = jnp.transpose(TS[...])
 
-    def halo_lane(f, p):
+    def unpack_both(level, slot, count):
+        for first, size in ((0, 3 * count), (3 * slab, count)):
+            TS[pl.ds(2 * first, size, stride=2), :] = RCU[level, slot, 1, pl.ds(first, size)]
+            TS[pl.ds(2 * first + 1, size, stride=2), :] = RCU[level, slot, 0, pl.ds(first, size)]
+        HT[slot] = jnp.transpose(TS[...])
+
+    def halo_lane(level, f, p):
         slot, q = (2, slab) if p == 0 else (0, p) if p <= slab else (1, p - slab)
-        return slot + (3 if f == 3 else 0), 2 * pair(f, q)
+        apart = f == 3 and (level < 3 or level == 3 and slot == 0)
+        return slot + (3 if apart else 0), 2 * pair(f, q)
 
     def sides(values, halo, at_lane):
         halo = pltpu.roll(halo, (2 * LANES - at_lane - 1) % LANES, 1)
@@ -255,7 +268,7 @@
         return behind, ahead
 
     def lateral(level, f, p, centre):
-        slot, at_lane = halo_lane(f, p)
+        slot, at_lane = halo_lane(level, f, p)
         for at, start in chunks:
             flat = pl.ds(start, CHUNK)
             values = UE[level, f, p, pl.ds(at, CHUNK), :]
@@ -292,7 +305,7 @@
         ready.add(key)
         return fresh
 
-    def sweep(level, base, hbase, offset, js, displace=True, relax=True):
+    def sweep(level, base, hbase, offset, js, displace=True, relax=True, gate=()):
         inside = range(base, base + slab)
         for p in range(min(js) + base - 1, max(js) + base + 2):
             centre = p - base in js
@@ -303,10 +316,11 @@
             for f in wanted:
                 if once("side", level, f, p):
                     lateral(level, f, p, p in inside)
-            if centre and displace:
-                for f in (1, 2):
-                    lateral_row(level, f, p, low, TOP - 1)
-                    lateral_row(level, f, p, high, TOP)
+        wires.receive(gate)
+        for p in (base + j for j in js if displace):
+            for f in (1, 2):
+                lateral_row(level, f, p, low, TOP - 1)
+                lateral_row(level, f, p, high, TOP)
 
         @each(js)
         def _(j):
@@ -479,9 +493,9 @@
     for p in (1, 2, 3, 4):
         derive(0, p, True)
     for level in range(3):
-        wires.receive(flat_u)
+        wires.receive(straight(flat_u))
         unpack(level, 0, 0, 3 * slab)
-        sweep(level, 1, 1, 0, (1, 2), relax=False)
+        sweep(level, 1, 1, 0, (1, 2), relax=False, gate=across(flat_u))
         pack_level(level + 1, (2, 3), (0, 1, 2))
         seen = set(ready)
         for core in (0, 1):
@@ -491,7 +505,8 @@
                 ready.clear()
                 ready.update(seen)
                 for right in (True, False) if core == 0 else (False, True):
-                    wires.receive([m for m in far_u if (m[0] < 0) == right])
+                    side = [m for m in far_u if (m[0] < 0) == right]
+                    wires.receive(straight(side))
                     if level == 0:
                         wires.receive([m for m in phase_far if (m[0] < 0) == right])
                         derive(0, 5 if right else 0, False)
@@ -499,7 +514,9 @@
                         unpack(level, 1, 0, 3)
                     else:
                         unpack(level, 2, 3 * (slab - 1), 3)
-                    sweep(level, 1, 1, 0, (3,) if right else (0,), relax=False)
+                    sweep(
+                        level, 1, 1, 0, (3,) if right else (0,), relax=False, gate=across(side)
+                    )
 
         pack_level(level + 1, (1, 4), (0, 1, 2))
         flat_u = send_flat_u(level + 1)
@@ -544,20 +561,16 @@
     for level in (3, 4, 5):
         hbase, offset = level - 1, level - 2
         if level > 3:
-            wires.receive(flat)
-            unpack(level, 0, 0, 3 * slab)
-            unpack(level, 0, 3 * slab, slab)
-        sweep(level, 2, hbase, offset, (0, 1))
+            wires.receive(straight(flat))
+            unpack_both(level, 0, slab)
+        sweep(level, 2, hbase, offset, (0, 1), gate=across(flat) if level > 3 else ())
         pack_level(level + 1, (1, 2))
         if level < 5:
             next_far = send_rims_back(level + 1)
-            next_far.append(planes(level + 1, every, 1, 5, -1))
-            next_far.append(planes(level + 1, 0, 2, 6, -1))
         else:
             next_far = [column(6, dz, 1, pl.ds(0, 3), -1) for dz in (-1, 1)]
             for dy in (-1, 1):
                 next_far.append(row(6, dy, pl.ds(1, 1), pl.ds(1, 1), pl.ds(5, 1), -1))
-            next_far.append(planes(6, every, 1, 5, -1))
         if level == 3:
             wires.receive(phase_far)
             unpack_phase(1, 1)
@@ -566,20 +579,21 @@
         elif level == 4:
             wires.receive(phase_later)
             derive(1, 7, True)
-        wires.receive(far)
-        unpack(level, 1, 0, 6)
-        unpack(level, 1, 3 * slab, 2)
+        wires.receive(straight(far))
+        unpack_both(level, 1, 2)
         if level == 5:
             derive(1, 8, True)
-        sweep(level, 2, hbase, offset, (2, 3))
+        sweep(level, 2, hbase, offset, (2, 3), gate=across(far))
         if level < 5:
             pack_level(level + 1, (3, 4))
             flat = send_flat_u(level + 1) + send_flat_v(level + 1)
-            next_far.append(planes(level + 1, pl.ds(1, 3), 2, 6, -1))
+            next_far.append(planes(level + 1, every, 1, 5, -1))
+            next_far.append(planes(level + 1, every, 2, 6, -1))
         else:
             pack_level(6, (3, 4), (0, 1, 2))
             flat = [column(6, dz, 0, u_pairs, 0) for dz in (-1, 1)]
             flat += [row(6, dy, pl.ds(1, 1), mine, mine, 0) for dy in (-1, 1)]
+            next_far.append(planes(6, every, 1, 5, -1))
             next_far.append(planes(6, 0, 2, 6, -1))
         far = next_far
 

time: 80.4 us -> 74.7 us (0.929)
  Pallas kernels: 79 us -> 73.8 us
    pallas_call x1, Pallas kernels: 77.9 us -> 72.7 us  [shards(): pl.pallas_call(functools.partial(kernel, ng, ny, nz), out_shape=jax.Shape...]
where the time goes in v5:
time: 74.7 us; the launch traced here: 74.6 us
  Pallas kernels  73.8 us (99%)
  between operations  0.8 us (1%)
    pallas_call x1, Pallas kernels, shards(): pl.pallas_call(functools.partial(kernel, ng, ny, nz), out_shape=jax.Shape...  72.7 us

profile of v5, /device:TPU:3, one launch (start us, length us, event | category | flops | bytes accessed | tf_op | source)
XLA Modules:
  0.0 74.6 jit_solution(1941637015992497417)
XLA Ops:
  0.6 72.7 %filament.1.packed = f32[5,4,128,128]{3,2,1,0:T(8,128)S(1)} custom-call(s32[4,128,128]{2,1,0:T(8,128)} %lab.1, f32[4,128,128]{2,1,0:T(8,128)} %rough.1, f32[4,128,128]{2,1,0:T(8,128)} %pot.1, f32[3,4,128,128]{3,2,1,0:T(8,128)} %disp.1), custom_call_target="tpu_custom_call" | custom-call | tf_op jit(solution)/shard_map/filament/pallas_call | solution.py:665
  73.4 1.1 %deliver.1 = (f32[4,128,128]{2,1,0:T(8,128)}, f32[4,128,128]{2,1,0:T(8,128)}, f32[3,4,128,128]{3,2,1,0:T(8,128)}) custom-call(f32[5,4,128,128]{3,2,1,0:T(8,128)S(1)} %filament.1.packed), custom_call_target="tpu_custom_call" | custom-call | tf_op jit(solution)/shard_map/deliver/pallas_call | solution.py:685

commit v6 on v5

--- a/solution.py
+++ b/solution.py
@@ -12,7 +12,7 @@
 TOP = 8
 CHUNK = 32
 LEVELS = 7
-COPIES = 173
+COPIES = 183
 
 
 class Wires:
@@ -62,7 +62,7 @@
     ng, ny, nz,
     lab, rough, pot, disp,
     out,
-    UE, CE, RCU, SCU, PH, RCP, SCP,
+    UE, CS, CR, RCU, SCU, PH, RCP, SCP,
     HH, CC, GZ, CZP, CZM, PZ, ZB, SB, PZP, PZM, TS, TT, HT, HP,
     LAB, ROU,
     send_sem, recv_sem, load_sem,
@@ -130,7 +130,7 @@
                 for f in range(4):
                     for p in (5, 6):
                         UE[level, f, p] = jnp.full(plane_shape, 1.0 if f == 3 else 0.0, f32)
-                CE[level, :, :, 4] = jnp.zeros((2, 3, 16, LANES), f32)
+                CR[level, pl.ds(4, 4)] = jnp.zeros((4, LANES), f32)
                 for side in range(2):
                     RCU[level, 1, side] = jnp.where(is_pot, 1.0, 0.0)
             PH[0, 5] = jnp.zeros(plane_shape, f32)
@@ -160,6 +160,18 @@
 
     def pack_level(level, planes, fields=(0, 1, 2, 3)):
         pack([(pair(f, q), UE, (level, f, q)) for q in planes for f in fields])
+        if 0 in fields:
+            mask = functools.reduce(
+                jnp.logical_or, [lane_row // 2 == pair(f, q) for q in planes for f in range(3)]
+            )
+            fresh = once("corner", level)
+            for end, at in enumerate((0, rows - 1)):
+                values = TS[pl.ds(at, 1), :]
+                if planes == (1, 2):
+                    CS[level, pl.ds(2 + end, 1), :] = values
+                if not fresh:
+                    values = jnp.where(mask, values, CS[level, pl.ds(end, 1), :])
+                CS[level, pl.ds(end, 1), :] = values
         for q in planes:
             for f in fields:
                 if f in (0, 3):
@@ -178,17 +190,16 @@
         )
 
     def straight(messages):
-        return [m for m in messages if not m[2]]
+        return [m for m in messages if m and not m[2]]
 
     def across(messages):
-        return [m for m in messages if m[2]]
-
-    def corner(level, dy, dz, here, there, dg):
-        src, dst = (TOP, TOP) if dy < 0 else (TOP + rows - 1, TOP - 1)
+        return [m for m in messages if m and m[2]]
+
+    def corner(level, dy, dz, kept, slot, dg):
+        src = kept + (0 if dy < 0 else 1)
+        dst = 4 * slot + (0 if dz > 0 else 2) + (0 if dy > 0 else 1)
         return wires.send(
-            UE.at[level, pl.ds(0, 3), here, pl.ds(src, 1)],
-            CE.at[level, 0 if dz > 0 else 1, :, there, pl.ds(dst, 1)],
-            dg, dy, dz,
+            CS.at[level, pl.ds(src, 1)], CR.at[level, pl.ds(dst, 1)], dg, dy, dz
         )
 
     def column(level, dz, slot, which, dg):
@@ -212,7 +223,7 @@
         for dy in (-1, 1):
             sent.append(row(level, dy, u_fields, mine, mine, 0))
             for dz in (-1, 1):
-                sent.append(corner(level, dy, dz, mine, pl.ds(0, slab), 0))
+                sent.append(corner(level, dy, dz, 0, 0, 0))
         return sent
 
     def send_flat_v(level):
@@ -233,16 +244,20 @@
     def send_both_ways_v(level):
         return [planes(level, 3, here, there, dg) for dg, here, there in ((-1, 1, 5), (1, 4, 0))]
 
-    def send_rims_back(level):
-        two = pl.ds(1, 2), pl.ds(5, 2)
-        sent = []
-        for dz in (-1, 1):
-            sent.append(column(level, dz, 1, pl.ds(0, 6), -1))
-            sent.append(column(level, dz, 1, pl.ds(3 * slab, 2), -1))
+    two_back = pl.ds(1, 2), pl.ds(5, 2)
+
+    def send_rims_back_u(level):
+        sent = [column(level, dz, 1, pl.ds(0, 6), -1) for dz in (-1, 1)]
         for dy in (-1, 1):
-            sent.append(row(level, dy, every, *two, -1))
+            sent.append(row(level, dy, u_fields, *two_back, -1))
             for dz in (-1, 1):
-                sent.append(corner(level, dy, dz, pl.ds(1, 1), pl.ds(4, 1), -1))
+                sent.append(corner(level, dy, dz, 0 if level == 3 else 2, 1, -1))
+        return sent
+
+    def send_back_v(level):
+        sent = [column(level, dz, 1, pl.ds(3 * slab, 2), -1) for dz in (-1, 1)]
+        sent += [row(level, dy, v_field, *two_back, -1) for dy in (-1, 1)]
+        sent.append(planes(level, 3, *two_back, -1))
         return sent
 
     def unpack(level, slot, first, size):
@@ -250,16 +265,9 @@
         TS[pl.ds(2 * first + 1, size, stride=2), :] = RCU[level, slot, 0, pl.ds(first, size)]
         HT[slot if first < 3 * slab else 3 + slot] = jnp.transpose(TS[...])
 
-    def unpack_both(level, slot, count):
-        for first, size in ((0, 3 * count), (3 * slab, count)):
-            TS[pl.ds(2 * first, size, stride=2), :] = RCU[level, slot, 1, pl.ds(first, size)]
-            TS[pl.ds(2 * first + 1, size, stride=2), :] = RCU[level, slot, 0, pl.ds(first, size)]
-        HT[slot] = jnp.transpose(TS[...])
-
-    def halo_lane(level, f, p):
+    def halo_lane(f, p):
         slot, q = (2, slab) if p == 0 else (0, p) if p <= slab else (1, p - slab)
-        apart = f == 3 and (level < 3 or level == 3 and slot == 0)
-        return slot + (3 if apart else 0), 2 * pair(f, q)
+        return slot + (3 if f == 3 else 0), 2 * pair(f, q)
 
     def sides(values, halo, at_lane):
         halo = pltpu.roll(halo, (2 * LANES - at_lane - 1) % LANES, 1)
@@ -268,7 +276,7 @@
         return behind, ahead
 
     def lateral(level, f, p, centre):
-        slot, at_lane = halo_lane(level, f, p)
+        slot, at_lane = halo_lane(f, p)
         for at, start in chunks:
             flat = pl.ds(start, CHUNK)
             values = UE[level, f, p, pl.ds(at, CHUNK), :]
@@ -281,14 +289,18 @@
                 if centre:
                     SB[f, p, flat, :] = ahead + behind
 
-    def lateral_row(level, f, p, at, corner_at):
+    def lateral_row(level, f, p, at, end):
+        slot, q = (0, p) if p <= slab else (1, p - slab)
+        k = pair(f, q)
         values = UE[level, f, p, pl.ds(at, 1), :]
-        left = CE[level, 0, f, p - 1, pl.ds(corner_at, 1), :]
-        right = CE[level, 1, f, p - 1, pl.ds(corner_at, 1), :]
-        behind = jnp.where(lane_row == 0, pltpu.roll(left, 1, 1), pltpu.roll(values, 1, 1))
+        left = CR[level, pl.ds(4 * slot + end, 1), :]
+        right = CR[level, pl.ds(4 * slot + 2 + end, 1), :]
+        behind = jnp.where(
+            lane_row == 0, pltpu.roll(left, (LANES - 2 * k) % LANES, 1), pltpu.roll(values, 1, 1)
+        )
         ahead = jnp.where(
             lane_row == LANES - 1,
-            pltpu.roll(right, LANES - 1, 1),
+            pltpu.roll(right, LANES - 2 - 2 * k, 1),
             pltpu.roll(values, LANES - 1, 1),
         )
         ZB[f, p, pl.ds(at, 1), :] = ahead - behind
@@ -319,8 +331,8 @@
         wires.receive(gate)
         for p in (base + j for j in js if displace):
             for f in (1, 2):
-                lateral_row(level, f, p, low, TOP - 1)
-                lateral_row(level, f, p, high, TOP)
+                lateral_row(level, f, p, low, 0)
+                lateral_row(level, f, p, high, 1)
 
         @each(js)
         def _(j):
@@ -505,10 +517,10 @@
                 ready.clear()
                 ready.update(seen)
                 for right in (True, False) if core == 0 else (False, True):
-                    side = [m for m in far_u if (m[0] < 0) == right]
+                    side = [m for m in far_u if m and (m[0] < 0) == right]
                     wires.receive(straight(side))
                     if level == 0:
-                        wires.receive([m for m in phase_far if (m[0] < 0) == right])
+                        wires.receive([m for m in phase_far if m and (m[0] < 0) == right])
                         derive(0, 5 if right else 0, False)
                     if right:
                         unpack(level, 1, 0, 3)
@@ -533,8 +545,8 @@
         if level < 2:
             far_v = send_both_ways_v(level + 1)
 
-    far = send_rims_back(3)
-    far.append(planes(3, pl.ds(1, 3), 1, 5, -1))
+    far_u = send_rims_back_u(3)
+    far_u.append(planes(3, pl.ds(1, 2), 1, 5, -1))
     wires.receive(flat_u)
     unpack(3, 0, 0, 3 * slab)
 
@@ -548,11 +560,10 @@
     phase_flat = send_phase_rims(1, 0)
     phase_far = send_phase_rims(1, -1)
     phase_far += send_phase_planes(1, ((-1, 1, 5, 2),))
-    far.append(planes(3, every, 2, 6, -1))
+    last_u = [planes(3, u_fields, 2, 6, -1)]
+    far_v = send_back_v(3)
     phase_later = send_phase_planes(1, ((-1, 3, 7, 2), (-2, 1, 9, 1)))
 
-    wires.receive(flat_v)
-    unpack(3, 0, 3 * slab, slab)
     wires.receive(phase_flat)
     unpack_phase(1, 0)
     derive(1, 1, False)
@@ -561,16 +572,18 @@
     for level in (3, 4, 5):
         hbase, offset = level - 1, level - 2
         if level > 3:
-            wires.receive(straight(flat))
-            unpack_both(level, 0, slab)
-        sweep(level, 2, hbase, offset, (0, 1), gate=across(flat) if level > 3 else ())
-        pack_level(level + 1, (1, 2))
+            wires.receive(straight(flat_u))
+            unpack(level, 0, 0, 3 * slab)
+        sweep(
+            level, 2, hbase, offset, (0, 1), relax=False, gate=across(flat_u) if level > 3 else ()
+        )
+        pack_level(level + 1, (1, 2), (0, 1, 2))
         if level < 5:
-            next_far = send_rims_back(level + 1)
+            next_u = send_rims_back_u(level + 1)
         else:
-            next_far = [column(6, dz, 1, pl.ds(0, 3), -1) for dz in (-1, 1)]
+            next_u = [column(6, dz, 1, pl.ds(0, 3), -1) for dz in (-1, 1)]
             for dy in (-1, 1):
-                next_far.append(row(6, dy, pl.ds(1, 1), pl.ds(1, 1), pl.ds(5, 1), -1))
+                next_u.append(row(6, dy, pl.ds(1, 1), pl.ds(1, 1), pl.ds(5, 1), -1))
         if level == 3:
             wires.receive(phase_far)
             unpack_phase(1, 1)
@@ -579,23 +592,34 @@
         elif level == 4:
             wires.receive(phase_later)
             derive(1, 7, True)
-        wires.receive(straight(far))
-        unpack_both(level, 1, 2)
+        wires.receive(straight(far_u))
+        unpack(level, 1, 0, 6)
         if level == 5:
             derive(1, 8, True)
-        sweep(level, 2, hbase, offset, (2, 3), gate=across(far))
+        sweep(level, 2, hbase, offset, (2,), relax=False, gate=across(far_u))
+        wires.receive(last_u)
+        sweep(level, 2, hbase, offset, (3,), relax=False)
+        pack_level(level + 1, (3, 4), (0, 1, 2))
         if level < 5:
-            pack_level(level + 1, (3, 4))
-            flat = send_flat_u(level + 1) + send_flat_v(level + 1)
-            next_far.append(planes(level + 1, every, 1, 5, -1))
-            next_far.append(planes(level + 1, every, 2, 6, -1))
+            flat_u = send_flat_u(level + 1)
         else:
-            pack_level(6, (3, 4), (0, 1, 2))
-            flat = [column(6, dz, 0, u_pairs, 0) for dz in (-1, 1)]
-            flat += [row(6, dy, pl.ds(1, 1), mine, mine, 0) for dy in (-1, 1)]
-            next_far.append(planes(6, every, 1, 5, -1))
-            next_far.append(planes(6, 0, 2, 6, -1))
-        far = next_far
+            flat_u = [column(6, dz, 0, u_pairs, 0) for dz in (-1, 1)]
+            flat_u += [row(6, dy, pl.ds(1, 1), mine, mine, 0) for dy in (-1, 1)]
+        next_u.append(planes(level + 1, u_fields, 1, 5, -1))
+        last_u = [planes(level + 1, u_fields if level < 5 else 0, 2, 6, -1)]
+        far_u = next_u
+
+        wires.receive(flat_v)
+        unpack(level, 0, 3 * slab, slab)
+        wires.receive(far_v)
+        unpack(level, 1, 3 * slab, 2)
+        sweep(level, 2, hbase, offset, (0, 1, 2, 3), displace=False)
+        if level < 5:
+            pack_level(level + 1, (1, 2, 3, 4), (3,))
+            flat_v = send_flat_v(level + 1)
+            far_v = send_back_v(level + 1)
+        else:
+            far_v = [planes(6, 3, 1, 5, -1)]
 
     def finish(j, at, start, value):
         out[0, j, pl.ds(start, CHUNK), :] = value
@@ -607,10 +631,12 @@
 
     for p in range(2, 5):
         hand_over(p)
-    wires.receive(flat)
+    wires.receive(flat_u)
     unpack(6, 0, 0, 3 * slab)
     phase_update(1, 6, 2, 5, 4, (0, 1), finish)
-    wires.receive(far)
+    wires.receive(far_u)
+    wires.receive(last_u)
+    wires.receive(far_v)
     unpack(6, 1, 0, 3)
     hand_over(5)
     phase_update(1, 6, 2, 5, 4, (2, 3), finish)
@@ -641,7 +667,8 @@
         hbm = pl.BlockSpec(memory_space=pltpu.HBM)
         scratch = [
             (LEVELS, 4, slab + 3, tall, lanes),
-            (LEVELS, 2, 3, slab + 1, 16, lanes),
+            (LEVELS, 8, lanes),
+            (LEVELS, 8, lanes),
             (LEVELS, 3, 2, 4 * slab, lanes),
             (LEVELS, 2, 4 * slab, lanes),
             (2, 10, tall, lanes),

time: 74.7 us -> 71.8 us (0.961)
  Pallas kernels: 73.8 us -> 70.9 us
    pallas_call x1, Pallas kernels: 72.7 us -> 69.8 us  [shards(): pl.pallas_call(functools.partial(kernel, ng, ny, nz), out_shape=jax.Shape...]
where the time goes in v6:
time: 71.8 us; the launch traced here: 71.7 us
  Pallas kernels  70.9 us (99%)
  between operations  0.8 us (1%)
    pallas_call x1, Pallas kernels, shards(): pl.pallas_call(functools.partial(kernel, ng, ny, nz), out_shape=jax.Shape...  69.8 us

profile of v6, /device:TPU:3, one launch (start us, length us, event | category | flops | bytes accessed | tf_op | source)
XLA Modules:
  0.0 71.7 jit_solution(7625246793456973225)
XLA Ops:
  0.6 69.8 %filament.1.packed = f32[5,4,128,128]{3,2,1,0:T(8,128)S(1)} custom-call(s32[4,128,128]{2,1,0:T(8,128)} %lab.1, f32[4,128,128]{2,1,0:T(8,128)} %rough.1, f32[4,128,128]{2,1,0:T(8,128)} %pot.1, f32[3,4,128,128]{3,2,1,0:T(8,128)} %disp.1), custom_call_target="tpu_custom_call" | custom-call | tf_op jit(solution)/shard_map/filament/pallas_call | solution.py:692
  70.4 1.1 %deliver.1 = (f32[4,128,128]{2,1,0:T(8,128)}, f32[4,128,128]{2,1,0:T(8,128)}, f32[3,4,128,128]{3,2,1,0:T(8,128)}) custom-call(f32[5,4,128,128]{3,2,1,0:T(8,128)S(1)} %filament.1.packed), custom_call_target="tpu_custom_call" | custom-call | tf_op jit(solution)/shard_map/deliver/pallas_call | solution.py:712

commit v7 on v6

--- a/solution.py
+++ b/solution.py
@@ -12,19 +12,23 @@
 TOP = 8
 CHUNK = 32
 LEVELS = 7
-COPIES = 183
+SENDS = 64
+LANDINGS = 131
 
 
 class Wires:
     def __init__(self, send_sem, recv_sem, place):
         self.send_sem, self.recv_sem = send_sem, recv_sem
         self.g, self.y, self.z, self.ng, self.ny, self.nz = place
-        self.count = 0
+        self.landings = 0
         self.pending = []
-
-    def send(self, src, dst, dg, dy, dz):
-        index = self.count
-        self.count += 1
+        self.keyed = {}
+
+    def send(self, src, dst, dg, dy, dz, key=None):
+        index = len(self.pending)
+        if index >= SENDS:
+            old_dg, old = self.pending[index - SENDS]
+            self.when_valid(old_dg, old.wait_send)
         target = (
             self.g + dg,
             lax.rem(self.y + dy + self.ny, self.ny),
@@ -33,14 +37,23 @@
         copy = pltpu.make_async_remote_copy(
             src_ref=src,
             dst_ref=dst,
-            send_sem=self.send_sem.at[index],
-            recv_sem=self.recv_sem.at[index],
+            send_sem=self.send_sem.at[index % SENDS],
+            recv_sem=self.recv_sem.at[self.landing(key)],
             device_id=target,
             device_id_type=MESH,
         )
         self.when_valid(dg, copy.start)
         self.pending.append((dg, copy))
         return (dg, copy, dy != 0)
+
+    def landing(self, key):
+        if key is not None:
+            uses = self.keyed.setdefault(key, [])
+            uses.append(uses[-2] if len(uses) > 1 else self.landings)
+            if len(uses) > 2:
+                return uses[-1]
+        self.landings += 1
+        return self.landings - 1
 
     def when_valid(self, dg, action):
         if dg == 0:
@@ -54,7 +67,7 @@
             self.when_valid(-dg, copy.wait_recv)
 
     def drain(self):
-        for dg, copy in self.pending:
+        for dg, copy in self.pending[-SENDS:]:
             self.when_valid(dg, copy.wait_send)
 
 
@@ -187,19 +200,21 @@
             UE.at[level, fields, here, pl.ds(src, 1)],
             UE.at[level, fields, there, pl.ds(dst, 1)],
             dg, dy, 0,
+            None if dg else ("row", dy, fields.start == 3),
         )
 
     def straight(messages):
-        return [m for m in messages if m and not m[2]]
+        return [m for m in messages if not m[2]]
 
     def across(messages):
-        return [m for m in messages if m and m[2]]
+        return [m for m in messages if m[2]]
 
     def corner(level, dy, dz, kept, slot, dg):
         src = kept + (0 if dy < 0 else 1)
         dst = 4 * slot + (0 if dz > 0 else 2) + (0 if dy > 0 else 1)
         return wires.send(
-            CS.at[level, pl.ds(src, 1)], CR.at[level, pl.ds(dst, 1)], dg, dy, dz
+            CS.at[level, pl.ds(src, 1)], CR.at[level, pl.ds(dst, 1)], dg, dy, dz,
+            None if dg else ("corner", dy, dz),
         )
 
     def column(level, dz, slot, which, dg):
@@ -207,6 +222,7 @@
             SCU.at[level, 0 if dz < 0 else 1, which],
             RCU.at[level, slot, 1 if dz < 0 else 0, which],
             dg, 0, dz,
+            None if dg else ("column", dz, which.start),
         )
 
     def planes(level, fields, here, there, dg):
@@ -328,11 +344,14 @@
             for f in wanted:
                 if once("side", level, f, p):
                     lateral(level, f, p, p in inside)
-        wires.receive(gate)
+        if not callable(gate):
+            wires.receive(gate)
         for p in (base + j for j in js if displace):
             for f in (1, 2):
                 lateral_row(level, f, p, low, 0)
                 lateral_row(level, f, p, high, 1)
+        if callable(gate):
+            gate()
 
         @each(js)
         def _(j):
@@ -428,26 +447,32 @@
         HP[slot] = jnp.transpose(TS[...])
 
     def derive(step, p, centre):
+        derive_own(step, p)
+        if centre:
+            derive_sides(step, p)
+
+    def derive_own(step, p):
+        for at, start in chunks:
+            h = h_of(PH[step, p, pl.ds(at, CHUNK), :])
+            HH[p, pl.ds(at, CHUNK), :] = 0.52 * h
+            CC[p, pl.ds(at, CHUNK), :] = 0.0075 + 0.0675 * h
+
+    def derive_sides(step, p):
         slot = 0 if p <= slab else 1
         for at, start in chunks:
             flat = pl.ds(start, CHUNK)
+            c = CC[p, pl.ds(at, CHUNK), :]
             phase = PH[step, p, pl.ds(at, CHUNK), :]
-            h = h_of(phase)
-            c = 0.0075 + 0.0675 * h
-            HH[p, pl.ds(at, CHUNK), :] = 0.52 * h
-            CC[p, pl.ds(at, CHUNK), :] = c
-            if centre:
-                behind, ahead = sides(phase, HP[slot, flat, :], 2 * (p - 1 - slot * slab))
-                h_behind, h_ahead = h_of(behind), h_of(ahead)
-                GZ[p, flat, :] = 0.52 * (h_ahead - h_behind)
-                CZP[p, flat, :] = c + (0.0075 + 0.0675 * h_ahead)
-                CZM[p, flat, :] = c + (0.0075 + 0.0675 * h_behind)
-                PZ[p, flat, :] = ahead + behind
-        if centre:
-            for at in (low, high):
-                h = h_of(PH[step, p, pl.ds(at, 1), :])
-                HH[p, pl.ds(at, 1), :] = 0.52 * h
-                CC[p, pl.ds(at, 1), :] = 0.0075 + 0.0675 * h
+            behind, ahead = sides(phase, HP[slot, flat, :], 2 * (p - 1 - slot * slab))
+            h_behind, h_ahead = h_of(behind), h_of(ahead)
+            GZ[p, flat, :] = 0.52 * (h_ahead - h_behind)
+            CZP[p, flat, :] = c + (0.0075 + 0.0675 * h_ahead)
+            CZM[p, flat, :] = c + (0.0075 + 0.0675 * h_behind)
+            PZ[p, flat, :] = ahead + behind
+        for at in (low, high):
+            h = h_of(PH[step, p, pl.ds(at, 1), :])
+            HH[p, pl.ds(at, 1), :] = 0.52 * h
+            CC[p, pl.ds(at, 1), :] = 0.0075 + 0.0675 * h
 
     def phase_update(step, level, base, hbase, offset, js, store):
         for j in js:
@@ -517,10 +542,10 @@
                 ready.clear()
                 ready.update(seen)
                 for right in (True, False) if core == 0 else (False, True):
-                    side = [m for m in far_u if m and (m[0] < 0) == right]
+                    side = [m for m in far_u if (m[0] < 0) == right]
                     wires.receive(straight(side))
                     if level == 0:
-                        wires.receive([m for m in phase_far if m and (m[0] < 0) == right])
+                        wires.receive([m for m in phase_far if (m[0] < 0) == right])
                         derive(0, 5 if right else 0, False)
                     if right:
                         unpack(level, 1, 0, 3)
@@ -564,18 +589,23 @@
     far_v = send_back_v(3)
     phase_later = send_phase_planes(1, ((-1, 3, 7, 2), (-2, 1, 9, 1)))
 
-    wires.receive(phase_flat)
-    unpack_phase(1, 0)
-    derive(1, 1, False)
-    for p in (2, 3, 4):
-        derive(1, p, True)
+    for p in (1, 2, 3, 4):
+        derive_own(1, p)
+
+    def phase_arrives():
+        wires.receive(phase_flat)
+        unpack_phase(1, 0)
+        derive_sides(1, 2)
+        derive_sides(1, 3)
+
     for level in (3, 4, 5):
         hbase, offset = level - 1, level - 2
         if level > 3:
             wires.receive(straight(flat_u))
             unpack(level, 0, 0, 3 * slab)
         sweep(
-            level, 2, hbase, offset, (0, 1), relax=False, gate=across(flat_u) if level > 3 else ()
+            level, 2, hbase, offset, (0, 1), relax=False,
+            gate=across(flat_u) if level > 3 else phase_arrives,
         )
         pack_level(level + 1, (1, 2), (0, 1, 2))
         if level < 5:
@@ -585,6 +615,7 @@
             for dy in (-1, 1):
                 next_u.append(row(6, dy, pl.ds(1, 1), pl.ds(1, 1), pl.ds(5, 1), -1))
         if level == 3:
+            derive_sides(1, 4)
             wires.receive(phase_far)
             unpack_phase(1, 1)
             derive(1, 5, True)
@@ -641,7 +672,7 @@
     hand_over(5)
     phase_update(1, 6, 2, 5, 4, (2, 3), finish)
     wires.drain()
-    assert wires.count == COPIES, wires.count
+    assert wires.landings == LANDINGS, wires.landings
 
 
 def deliver(packed, phase, potential, displacement, sem):
@@ -698,8 +729,8 @@
             + [
                 pltpu.VMEM(labels.shape, jnp.int32),
                 pltpu.VMEM(labels.shape, f32),
-                pltpu.SemaphoreType.DMA((COPIES,)),
-                pltpu.SemaphoreType.DMA((COPIES,)),
+                pltpu.SemaphoreType.DMA((SENDS,)),
+                pltpu.SemaphoreType.DMA((LANDINGS,)),
                 pltpu.SemaphoreType.DMA((4,)),
             ],
             compiler_params=pltpu.CompilerParams(

time: 71.8 us -> 70.4 us (0.981)
  Pallas kernels: 70.9 us -> 69.5 us
    pallas_call x1, Pallas kernels: 69.8 us -> 68.4 us  [shards(): pl.pallas_call(functools.partial(kernel, ng, ny, nz), out_shape=jax.Shape...]
where the time goes in v7:
time: 70.4 us; the launch traced here: 70.3 us
  Pallas kernels  69.5 us (99%)
  between operations  0.8 us (1%)
    pallas_call x1, Pallas kernels, shards(): pl.pallas_call(functools.partial(kernel, ng, ny, nz), out_shape=jax.Shape...  68.4 us

profile of v7, /device:TPU:3, one launch (start us, length us, event | category | flops | bytes accessed | tf_op | source)
XLA Modules:
  0.0 70.3 jit_solution(455991367997634054)
XLA Ops:
  0.6 68.4 %filament.1.packed = f32[5,4,128,128]{3,2,1,0:T(8,128)S(1)} custom-call(s32[4,128,128]{2,1,0:T(8,128)} %lab.1, f32[4,128,128]{2,1,0:T(8,128)} %rough.1, f32[4,128,128]{2,1,0:T(8,128)} %pot.1, f32[3,4,128,128]{3,2,1,0:T(8,128)} %disp.1), custom_call_target="tpu_custom_call" | custom-call | tf_op jit(solution)/shard_map/filament/pallas_call | solution.py:723
  69.0 1.1 %deliver.1 = (f32[4,128,128]{2,1,0:T(8,128)}, f32[4,128,128]{2,1,0:T(8,128)}, f32[3,4,128,128]{3,2,1,0:T(8,128)}) custom-call(f32[5,4,128,128]{3,2,1,0:T(8,128)S(1)} %filament.1.packed), custom_call_target="tpu_custom_call" | custom-call | tf_op jit(solution)/shard_map/deliver/pallas_call | solution.py:743

commit v8 on v7

--- a/solution.py
+++ b/solution.py
@@ -12,8 +12,8 @@
 TOP = 8
 CHUNK = 32
 LEVELS = 7
-SENDS = 64
-LANDINGS = 131
+SENDS = 32
+LANDINGS = 119
 
 
 class Wires:
@@ -92,8 +92,7 @@
     barrier = pltpu.get_barrier_semaphore()
     around = [(a, b) for a in (-1, 0, 1) for b in (-1, 0, 1)]
     partners = [(0, a, b) for a, b in around if (a, b) != (0, 0)]
-    partners += [(s, a, b) for s in (-1, 1) for a, b in around]
-    partners += [(-2, 0, 0), (2, 0, 0)]
+    partners += [(s, a, b) for s in (-1, 1) for a, b in around if a * b == 0]
     for dg, dy, dz in partners:
         def greet(dg=dg, dy=dy, dz=dz):
             pl.semaphore_signal(
@@ -200,7 +199,7 @@
             UE.at[level, fields, here, pl.ds(src, 1)],
             UE.at[level, fields, there, pl.ds(dst, 1)],
             dg, dy, 0,
-            None if dg else ("row", dy, fields.start == 3),
+            ("row", dy, fields.start == 3, dg) if dg == 0 or level < 3 else None,
         )
 
     def straight(messages):
@@ -222,12 +221,13 @@
             SCU.at[level, 0 if dz < 0 else 1, which],
             RCU.at[level, slot, 1 if dz < 0 else 0, which],
             dg, 0, dz,
-            None if dg else ("column", dz, which.start),
+            ("column", dz, which.start, dg) if dg == 0 or level < 3 else None,
         )
 
     def planes(level, fields, here, there, dg):
         return wires.send(
-            UE.at[level, fields, here, own], UE.at[level, fields, there, own], dg, 0, 0
+            UE.at[level, fields, here, own], UE.at[level, fields, there, own], dg, 0, 0,
+            ("plane", dg, fields == 3) if level < 3 else None,
         )
 
     every, mine = pl.ds(0, 4), pl.ds(1, slab)
@@ -510,18 +510,19 @@
 
     count = len([p for p in partners if p[0] == 0])
     total = count + sum(
-        9 * jnp.where(ok, 1, 0) for ok in (g > 0, g < ng - 1)
-    ) + sum(jnp.where(ok, 1, 0) for ok in (g > 1, g < ng - 2))
+        5 * jnp.where(ok, 1, 0) for ok in (g > 0, g < ng - 1)
+    )
     pack_phase(0)
     loads[0].wait()
     loads[1].wait()
-    pack_level(0, (1, 2, 3, 4))
+    pack_level(0, (1, 2, 3, 4), (0, 1, 2))
     pl.semaphore_wait(barrier, total)
 
     phase_flat = send_phase_rims(0, 0)
     flat_u = send_flat_u(0)
+    far_u = send_both_ways_u(0)
+    pack_level(0, (1, 2, 3, 4), (3,))
     flat_v = send_flat_v(0)
-    far_u = send_both_ways_u(0)
     phase_far = send_phase_planes(0, ((-1, 1, 5, 1), (1, 4, 0, 1)))
     far_v = send_both_ways_v(0)
     pin_outside()

time: 70.4 us -> 69.1 us (0.982)
  Pallas kernels: 69.5 us -> 68 us
    pallas_call x1, Pallas kernels: 68.4 us -> 66.9 us  [shards(): pl.pallas_call(functools.partial(kernel, ng, ny, nz), out_shape=jax.Shape...]
where the time goes in v8:
time: 69.1 us; the launch traced here: 68.8 us
  Pallas kernels  68 us (98%)
  between operations  0.8 us (1%)
    pallas_call x1, Pallas kernels, shards(): pl.pallas_call(functools.partial(kernel, ng, ny, nz), out_shape=jax.Shape...  66.9 us

profile of v8, /device:TPU:3, one launch (start us, length us, event | category | flops | bytes accessed | tf_op | source)
XLA Modules:
  0.0 68.8 jit_solution(14222729792444936885)
XLA Ops:
  0.6 66.9 %filament.1.packed = f32[5,4,128,128]{3,2,1,0:T(8,128)S(1)} custom-call(s32[4,128,128]{2,1,0:T(8,128)} %lab.1, f32[4,128,128]{2,1,0:T(8,128)} %rough.1, f32[4,128,128]{2,1,0:T(8,128)} %pot.1, f32[3,4,128,128]{3,2,1,0:T(8,128)} %disp.1), custom_call_target="tpu_custom_call" | custom-call | tf_op jit(solution)/shard_map/filament/pallas_call | solution.py:724
  67.5 1.1 %deliver.1 = (f32[4,128,128]{2,1,0:T(8,128)}, f32[4,128,128]{2,1,0:T(8,128)}, f32[3,4,128,128]{3,2,1,0:T(8,128)}) custom-call(f32[5,4,128,128]{3,2,1,0:T(8,128)S(1)} %filament.1.packed), custom_call_target="tpu_custom_call" | custom-call | tf_op jit(solution)/shard_map/deliver/pallas_call | solution.py:744
